TPU v7x, 768 devices: a whole 4x8x12 slice. The times are simulated.
768 devices in a mesh: blk: 16 (over y, x_hi), grp: 48 (over z, x_lo, core).
Axes of the slice: x: 4 (x_hi: 2, x_lo: 2; x = x_hi * 2 + x_lo), y: 8, z: 12, core: 2. Of those that a mesh axis runs over, the one named last changes fastest.
Arguments:
- field: float32 [768, 768, 512], P('grp', 'blk'), may hold values from -7 to 7
- x_panel: float32 [768, 144], P('blk'), as said below
- y_factor: float32 [768, 768], replicated, as said below
- z_factor: float32 [512, 512], replicated, as said below
- scaling: float32 [768, 768, 512], P('grp', 'blk'), may hold values from 0.3 to 3
Outputs:
- updated: float32 [768, 768, 512], P('grp', 'blk')
Inputs may be any that keep to these rules, and one draw needn't show every extreme that they name: x_panel[x, j] is zero where j - 48 - (x mod 48) lies outside -48 to 48. y_factor[i, k] is zero where the periodic distance of i and k exceeds 48. z_factor[i, k] is zero where the periodic distance of i and k exceeds 48.
All inputs are finite; a program needn't handle non-finite values.
Results may differ from a plain program's by a relative error of at most 0.0003.
Values sent between devices are 32-bit elements; how exact they have to be, the bound alone decides.
No kernel may reach another device: no remote copies, remote signals or barrier semaphores. Data moves between devices by JAX's collectives and lax.ppermute only.
A program may use at most 32 MiB of HBM per device.

v0:
```python
import jax
import jax.numpy as jnp
from jax import lax
from jax.sharding import PartitionSpec as P

HOR = 48


def padded(cells, sides, width):
    for axis, dim in sides:
        count = lax.axis_size(axis)
        head = lax.slice_in_dim(cells, 0, width, axis=dim)
        tail = lax.slice_in_dim(cells, cells.shape[dim] - width, cells.shape[dim], axis=dim)
        cells = jnp.concatenate(
            [
                lax.ppermute(tail, axis, [(i, (i + 1) % count) for i in range(count)]),
                cells,
                lax.ppermute(head, axis, [((i + 1) % count, i) for i in range(count)]),
            ],
            axis=dim,
        )
    return cells


def apply_depth(block, z_factor):
    return lax.dot_general(
        block, z_factor, (((2,), (1,)), ((), ())), precision=lax.Precision.HIGHEST
    )


def apply_planes(x_panel, widened):
    return jnp.einsum("rj,yjz->yrz", x_panel, widened, precision=lax.Precision.HIGHEST)


def apply_across(block, y_factor):
    rows_here, planes, cells = block.shape
    flat = block.reshape(rows_here, planes * cells)
    pencils = lax.all_to_all(flat, "grp", split_axis=1, concat_axis=0, tiled=True)
    turned = jnp.dot(y_factor, pencils, precision=lax.Precision.HIGHEST)
    back = lax.all_to_all(turned, "grp", split_axis=0, concat_axis=1, tiled=True)
    return back.reshape(rows_here, planes, cells)


def on_device(field, x_panel, y_factor, z_factor, scaling):
    depth = apply_depth(field, z_factor)
    across = apply_across(depth, y_factor)
    widened = padded(across, (("blk", 1),), HOR)
    along = apply_planes(x_panel, widened)
    return along * scaling


def solution(mesh):
    in_specs = (P("grp", "blk", None), P("blk", None), P(), P(), P("grp", "blk", None))
    out_specs = P("grp", "blk", None)
    return jax.shard_map(
        on_device, mesh=mesh, in_specs=in_specs, out_specs=out_specs, check_vma=False
    )
```

profile of v0, /device:TPU:61, one launch (start us, length us, event | category | flops | bytes accessed | tf_op | source)
XLA Modules:
  0.0 235.4 jit_solution(9582780709460408581)
XLA Ops:
  0.0 0.0 copy-start
  0.0 5.3 %fusion.6 = f32[16,48,512]{2,0,1:T(8,128)S(1)} fusion(f32[16,48,512]{2,1,0:T(8,128)} %param.5, f32[512,512]{1,0:T(8,128)} %param.8), kind=kOutput, calls=%fused_computation.7 | convolution fusion | flops 2415919104 | bytes 4194304 | tf_op jit(solution)/shard_map/dot_general | solution.py:26
  5.3 75.5 %all_to_all.32 = f32[16,48,512]{2,0,1:T(8,128)S(1)} all-to-all(f32[16,48,512]{2,0,1:T(8,128)S(1)} %fusion.6), channel_id=1, replica_groups=mesh['blk'=16,'grp'=48] {'grp'}, dimensions={1} | all-to-all | bytes 3145728 | tf_op jit(solution)/shard_map/all_to_all | solution.py:38
  80.8 0.0 copy-done
  80.8 8.8 %convolution_bitcast_fusion = f32[768,512]{0,1:T(8,128)} fusion(f32[768,512]{1,0:T(8,128)S(1)} %bitcast.20, f32[768,768]{1,0:T(8,128)S(1)} %copy-done), kind=kOutput, calls=%fused_computation.10 | convolution fusion | flops 3623878656 | bytes 5505024 | tf_op jit(solution)/shard_map/dot_general | solution.py:39
  89.6 3.0 %copy.11 = f32[768,512]{1,0:T(8,128)} copy(f32[768,512]{0,1:T(8,128)} %convolution_bitcast_fusion) | data formatting | bytes 3145728 | tf_op jit(solution)/shard_map/dot_general | solution.py:39
  92.7 63.1 %all_to_all.33 = f32[48,16,512]{2,1,0:T(8,128)S(1)} all-to-all(f32[48,16,512]{2,1,0:T(8,128)} %bitcast.19), channel_id=1, replica_groups=mesh['blk'=16,'grp'=48] {'grp'}, dimensions={0} | all-to-all | bytes 3145728 | tf_op jit(solution)/shard_map/all_to_all | solution.py:40
  155.8 0.0 copy-start.1
  155.8 0.0 copy-start.2
  155.8 0.9 copy.18
  156.7 2.4 %collective-permute-start.1 = (f32[16,48,512]{2,1,0:T(8,128)S(1)}, f32[16,48,512]{2,1,0:T(8,128)S(1)}, u32[]{:S(2)}, u32[]{:S(2)}) collective-permute-start(f32[16,48,512]{2,1,0:T(8,128)S(1)} %bitcast.21), channel_id=1, source_target_pairs={{48,0},{96,48},{144,96},{192,144},{240,192},{288,240},{336,288},{3... | collective-permute-start | bytes 4718600 | tf_op jit(solution)/shard_map/ppermute | solution.py:18
  159.2 6.5 %collective-permute-start = (f32[16,48,512]{2,1,0:T(8,128)S(1)}, f32[16,48,512]{2,1,0:T(8,128)S(1)}, u32[]{:S(2)}, u32[]{:S(2)}) collective-permute-start(f32[16,48,512]{2,1,0:T(8,128)S(1)} %bitcast.22), channel_id=1, source_target_pairs={{0,48},{48,96},{96,144},{144,192},{192,240},{240,288},{288,336},{3... | collective-permute-start | bytes 4718600 | tf_op jit(solution)/shard_map/ppermute | solution.py:16
  165.6 60.6 %collective-permute-done.1 = f32[16,48,512]{2,1,0:T(8,128)S(1)} collective-permute-done((f32[16,48,512]{2,1,0:T(8,128)S(1)}, f32[16,48,512]{2,1,0:T(8,128)S(1)}, u32[]{:S(2)}, u32[]{:S(2)}) %collective-permute-start.1) | collective-permute-done | bytes 1572896 | tf_op jit(solution)/shard_map/ppermute | solution.py:18
  226.2 5.2 %collective-permute-done = f32[16,48,512]{2,1,0:T(8,128)S(1)} collective-permute-done((f32[16,48,512]{2,1,0:T(8,128)S(1)}, f32[16,48,512]{2,1,0:T(8,128)S(1)}, u32[]{:S(2)}, u32[]{:S(2)}) %collective-permute-start) | collective-permute-done | bytes 1572896 | tf_op jit(solution)/shard_map/ppermute | solution.py:16
  231.4 0.0 copy-done.1
  231.4 0.0 copy-done.2
  231.4 4.0 %bitcast_multiply_fusion = f32[16,48,512]{2,1,0:T(8,128)} fusion(f32[16,48,512]{2,1,0:T(8,128)S(1)} %copy-done.1, f32[16,48,512]{2,1,0:T(8,128)S(1)} %collective-permute-done.1, f32[16,48,512]{2,1,0:T(8,128)S(1)} %bitcast.23, f32[16,48,512]{2,1,0:T(8,128)S(1)} %collective-permute-done, f32[48,144]{1,0:T(8,128)S(1)} %copy-done.2), kind=kOutput, calls=%fused_computation.6 | convolution fusion | flops 682229760 | bytes 7891968 | tf_op jit(solution)/shard_map/rj,yjz->yrz/dot_general | solution.py:32
Async XLA Ops:
  0.0 80.8 %copy-start = (f32[768,768]{1,0:T(8,128)S(1)}, f32[768,768]{1,0:T(8,128)}, u32[]{:S(2)}) copy-start(f32[768,768]{1,0:T(8,128)} %param.7) | copy-start | bytes 7077892
  155.8 75.6 %copy-start.1 = (f32[16,48,512]{2,1,0:T(8,128)S(1)}, f32[16,48,512]{2,1,0:T(8,128)}, u32[]{:S(2)}) copy-start(f32[16,48,512]{2,1,0:T(8,128)} %param.9) | copy-start | bytes 4718596
  155.8 75.6 %copy-start.2 = (f32[48,144]{1,0:T(8,128)S(1)}, f32[48,144]{1,0:T(8,128)}, u32[]{:S(2)}) copy-start(f32[48,144]{1,0:T(8,128)} %param.6) | copy-start | bytes 82948
  156.7 69.5 %collective-permute-start.1 = (f32[16,48,512]{2,1,0:T(8,128)S(1)}, f32[16,48,512]{2,1,0:T(8,128)S(1)}, u32[]{:S(2)}, u32[]{:S(2)}) collective-permute-start(f32[16,48,512]{2,1,0:T(8,128)S(1)} %bitcast.21), channel_id=1, source_target_pairs={{48,0},{96,48},{144,96},{192,144},{240,192},{288,240},{336,288},{3... | collective-permute-start | bytes 4718600 | tf_op jit(solution)/shard_map/ppermute | solution.py:18
  159.2 72.2 %collective-permute-start = (f32[16,48,512]{2,1,0:T(8,128)S(1)}, f32[16,48,512]{2,1,0:T(8,128)S(1)}, u32[]{:S(2)}, u32[]{:S(2)}) collective-permute-start(f32[16,48,512]{2,1,0:T(8,128)S(1)} %bitcast.22), channel_id=1, source_target_pairs={{0,48},{48,96},{96,144},{144,192},{192,240},{240,288},{288,336},{3... | collective-permute-start | bytes 4718600 | tf_op jit(solution)/shard_map/ppermute | solution.py:16
where the time goes:
time: 236 us; the launch traced here: 235 us
  blocking collectives  139 us (59%)
  waiting for transfers between devices  65.8 us (28%)
  matrix products  18.1 us (8%)
  starting transfers between devices  8.9 us (4%)
  local copies, waits for them, and re-layouts  3.97 us (2%)
    all_to_all x1, blocking collectives, apply_across(): lax.all_to_all(flat, 'grp', split_axis=1, concat_axis=0, tiled=True)  75.5 us
    all_to_all x1, blocking collectives, apply_across(): lax.all_to_all(turned, 'grp', split_axis=0, concat_axis=1, tiled=True)  63.1 us
    ppermute x1, waiting for transfers between devices, padded(): lax.ppermute(head, axis, [((i + 1) % count, i) for i in range(count)])  60.6 us
    dot_general x1, matrix products, apply_across(): turned = jnp.dot(y_factor, pencils, precision=lax.Precision.HIGHEST)  8.8 us
    ppermute x1, starting transfers between devices, padded(): lax.ppermute(tail, axis, [(i, (i + 1) % count) for i in range(count)])  6.47 us
    dot_general x1, matrix products, apply_depth(): lax.dot_general(block, z_factor, (((2,), (1,)), ((), ())), precision=lax....  5.28 us
    ppermute x1, waiting for transfers between devices, padded(): lax.ppermute(tail, axis, [(i, (i + 1) % count) for i in range(count)])  5.21 us
  transfers between devices with their start and end apart: 2, of which 2 were waited for; matrix products, arithmetic and copies ran while one was open for 0% of the time, Pallas kernels for 0%

commit v1 on v0

v1 whole, which is shorter than its diff:
```python
import functools

import jax
import jax.numpy as jnp
from jax import lax
from jax.experimental import pallas as pl
from jax.experimental.pallas import tpu as pltpu
from jax.sharding import PartitionSpec as P

AXES = ("blk", "grp")
ROWS = 384
EXTRA = 24
INTERPRET = False


def split(v):
    hi = v.astype(jnp.bfloat16)
    return hi, (v - hi.astype(jnp.float32)).astype(jnp.bfloat16)


def dot3(a, b, dims):
    (ah, al), (bh, bl) = a, b
    mul = lambda p, q: lax.dot_general(p, q, (dims, ((), ())), preferred_element_type=jnp.float32)
    return mul(ah, bh) + (mul(ah, bl) + mul(al, bh))


def halves(a, b, low):
    return jnp.where(low, a, pltpu.roll(b, 64, 1)), jnp.where(low, pltpu.roll(a, 64, 1), b)


def low_lanes(rows):
    return lax.broadcasted_iota(jnp.int32, (rows, 128), 1) < 64


def depth_kernel(field_ref, z_ref, extra_ref, out_ref):
    for d in range(8):
        out_ref[d, pl.ds(ROWS, EXTRA), :] = extra_ref[...]
    for u in range(2):
        zs = split(z_ref[pl.ds(256 * u, 256), :])
        for m in range(4):
            ys = (2 * m, 2 * m + 1, 8 + 2 * m, 9 + 2 * m)
            rows = jnp.concatenate([field_ref[pl.ds(48 * y, 48), :] for y in ys], axis=0)
            t = dot3(split(rows), zs, ((1,), (1,)))
            for v in range(2):
                tile = t[:, 128 * v : 128 * v + 128]
                d = 2 * (2 * u + v)
                for i, y in enumerate(ys):
                    part = tile[48 * i : 48 * i + 48]
                    e = jnp.where(low_lanes(24), part[:24], pltpu.roll(part[24:], 64, 1))
                    out_ref[d, pl.ds(y, 24, stride=16), :] = e
                for i in range(2):
                    a = tile[48 * i : 48 * i + 48]
                    b = tile[96 + 48 * i : 144 + 48 * i]
                    o = jnp.where(low_lanes(48), pltpu.roll(a, 64, 1), b)
                    out_ref[d + 1, pl.ds(48 * ys[i], 48), :] = o


def y_pass(own, up, down, ym, emit):
    ys = split(ym[...])
    for xh in range(2):
        def step(i, carry):
            cols = []
            for j in range(2):
                at = pl.ds(pl.multiple_of((2 * i + j) * 16, 16), 16)
                cols.append(
                    jnp.concatenate(
                        [up[3 * xh + s, at, :] for s in range(3)]
                        + [own[4 * xh + s, at, :] for s in range(4)]
                        + [down[3 * xh + s, at, :] for s in range(3)],
                        axis=0,
                    )
                )
            r = dot3(ys, split(jnp.concatenate(cols, axis=1)), ((1,), (0,)))
            for j in range(2):
                emit(xh, 2 * i + j, r[:, 128 * j : 128 * j + 128])
            return carry

        lax.fori_loop(0, 12, step, 0)


def x_pass(own, left, right, xm, emit):
    xs = split(xm[...])
    for s in range(4):
        def step(i, carry):
            cols = []
            for j in range(2):
                at = pl.ds(pl.multiple_of((2 * i + j) * 48, 16), 48)
                cols.append(
                    jnp.concatenate(
                        [left[s, at, :], own[s, at, :], own[4 + s, at, :], right[s, at, :]], axis=0
                    )
                )
            r = dot3(xs, split(jnp.concatenate(cols, axis=1)), ((1,), (0,)))
            for j in range(2):
                emit(s, 2 * i + j, r[:, 128 * j : 128 * j + 128])
            return carry

        lax.fori_loop(0, 4, step, 0)


def first_kernel(core_ref, own, lo, hi, ym, xm, out, plus, minus):
    core = core_ref[0]

    @pl.when(core == 0)
    def _():
        def emit(xh, xx, r):
            for s in range(4):
                w = halves(r[16 * s : 16 * s + 8], r[16 * s + 8 : 16 * s + 16], low_lanes(8))
                for h in range(2):
                    out[4 * xh + s, pl.ds(24 * h + xx, 8, stride=48), :] = w[h]

        y_pass(own, lo, hi, ym, emit)
        for s in range(4):
            plus[s] = out[4 + s]
            minus[s] = out[s]

    @pl.when(core == 1)
    def _():
        def emit(s, yy, r):
            for xh in range(2):
                p = r[48 * xh : 48 * xh + 48]
                q = halves(p[:24], p[24:], low_lanes(24))
                for yh in range(2):
                    out[4 * xh + s, pl.ds(8 * yh + yy, 24, stride=16), :] = q[yh]

        x_pass(own, lo, hi, xm, emit)
        for xh in range(2):
            for s in range(3):
                plus[3 * xh + s] = out[4 * xh + s + 1]
                minus[3 * xh + s] = out[4 * xh + s]


def second_kernel(core_ref, own, lo, hi, ym, xm, out):
    core = core_ref[0]

    @pl.when(core == 0)
    def _():
        def emit(s, yy, r):
            for xh in range(2):
                out[4 * xh + s, pl.ds(pl.multiple_of(48 * yy, 16), 48), :] = r[48 * xh : 48 * xh + 48]

        x_pass(own, lo, hi, xm, emit)

    @pl.when(core == 1)
    def _():
        def emit(xh, xx, r):
            for s in range(4):
                out[4 * xh + s, pl.ds(pl.multiple_of(16 * xx, 16), 16), :] = r[16 * s : 16 * s + 16]

        y_pass(own, lo, hi, ym, emit)


def last_kernel(got, scale_ref, out_ref):
    low = low_lanes(24)
    for t in range(4):
        lanes = pl.ds(128 * t, 128)
        for yy in range(8):
            a = got[2 * t, pl.ds(48 * yy, 48), :]
            for yh in range(2):
                y = 8 * yh + yy
                c = got[2 * t + 1, pl.ds(y, 24, stride=16), :]
                c2 = pltpu.roll(c, 64, 1)
                a2 = pltpu.roll(a, 64, 1) if yh else a
                for h in range(2):
                    at = pl.ds(48 * y + 24 * h, 24)
                    r = jnp.where(low, a2[24 * h : 24 * h + 24], c if h else c2)
                    out_ref[at, lanes] = r * scale_ref[at, lanes]


def call(kernel, shapes, *args, scalar=False):
    specs = [pl.BlockSpec(memory_space=pltpu.VMEM) for _ in args]
    if scalar:
        specs[0] = pl.BlockSpec(memory_space=pltpu.SMEM)
    return pl.pallas_call(
        kernel,
        out_shape=[jax.ShapeDtypeStruct(s, jnp.float32) for s in shapes],
        in_specs=specs,
        out_specs=[pl.BlockSpec(memory_space=pltpu.VMEM) for _ in shapes],
        interpret=INTERPRET,
    )(*args)


def links(mesh):
    n_blk, n_grp = mesh.shape["blk"], mesh.shape["grp"]
    n_y, n_z = n_blk // 2, n_grp // 4

    def place(y, xh, z, r):
        return ((y % n_y) * 2 + xh) * n_grp + (z % n_z) * 4 + r

    everyone = [(y, xh, z, r) for y in range(n_y) for xh in range(2) for z in range(n_z) for r in range(4)]

    def hop(step, along_z):
        pairs = []
        for y, xh, z, r in everyone:
            if r % 2 == along_z:
                to = place(y, xh, z + step, r)
            else:
                to = place(y + step, xh, z, r)
            pairs.append((place(y, xh, z, r), to))
        return pairs

    eights = [[place(y, xh, z, r) for xh in range(2) for r in range(4)] for y in range(n_y) for z in range(n_z)]
    return eights, hop


def on_device(eights, hop, field, x_panel, y_factor, z_factor, scaling):
    grp = lax.axis_index("grp")
    core = grp % 2
    slab, share = grp // 4, grp % 4
    ny = y_factor.shape[0]

    quarter = lax.dynamic_slice_in_dim(x_panel, 12 * share, 12, 0)
    extra = jnp.concatenate([quarter[:, :128], jnp.pad(quarter[:, 128:], ((0, 0), (0, 112)))], axis=0)
    band = lax.dynamic_slice_in_dim(y_factor, 64 * slab, 64, 0)
    band = jnp.concatenate([band[:, ny - 48 :], band, band[:, :64]], axis=1)
    ym = lax.dynamic_slice_in_dim(band, 64 * slab, 160, 1)

    (sent,) = call(depth_kernel, [(8, ROWS + EXTRA, 128)], field.reshape(768, 512), z_factor, extra)
    got = lax.all_to_all(sent, AXES, split_axis=0, concat_axis=0, tiled=True, axis_index_groups=eights)

    tail = got[:, ROWS:, :]
    panel = jnp.concatenate([tail[:, :12], tail[:, 12:, :16]], axis=2).reshape(2, 48, 144)
    xm = jnp.concatenate(
        [jnp.pad(panel[0], ((0, 0), (0, 48))), jnp.pad(panel[1], ((0, 0), (48, 0)))], axis=0
    )
    own = got[:, :ROWS, :]

    def pick(first, second):
        at = jnp.where(core == 0, jnp.array(first), jnp.array(second))
        return jnp.concatenate([lax.dynamic_slice_in_dim(own, at[i], 1, 0) for i in range(6)], axis=0)

    plus = pick((1, 2, 3, 5, 6, 7), (4, 5, 6, 7, 7, 7))
    minus = pick((0, 1, 2, 4, 5, 6), (0, 1, 2, 3, 3, 3))
    lo = lax.ppermute(plus, AXES, hop(1, 0))
    hi = lax.ppermute(minus, AXES, hop(-1, 0))
    flag = core.astype(jnp.int32).reshape(1)
    own, plus, minus = call(
        first_kernel,
        [(8, ROWS, 128), (6, ROWS, 128), (6, ROWS, 128)],
        flag, own, lo, hi, ym, xm, scalar=True,
    )
    lo = lax.ppermute(plus, AXES, hop(1, 1))
    hi = lax.ppermute(minus, AXES, hop(-1, 1))
    (sent,) = call(second_kernel, [(8, ROWS, 128)], flag, own, lo, hi, ym, xm, scalar=True)
    got = lax.all_to_all(sent, AXES, split_axis=0, concat_axis=0, tiled=True, axis_index_groups=eights)
    (out,) = call(last_kernel, [(768, 512)], got, scaling.reshape(768, 512))
    return out.reshape(16, 48, 512)


def solution(mesh):
    eights, hop = links(mesh)
    in_specs = (P("grp", "blk", None), P("blk", None), P(), P(), P("grp", "blk", None))
    return jax.shard_map(
        functools.partial(on_device, eights, hop),
        mesh=mesh,
        in_specs=in_specs,
        out_specs=P("grp", "blk", None),
        check_vma=False,
    )
```

time: 236 us -> 147 us (0.62)
  the two profiles are of different devices: /device:TPU:61 before, /device:TPU:24 now
where the time goes in v1:
time: 147 us; the launch traced here: 146 us
  waiting for transfers between devices  31.2 us (21%)
  starting transfers between devices  27.5 us (19%)
  blocking collectives  26.5 us (18%)
  Pallas kernels  25.5 us (17%)
  between operations  22.4 us (15%)
  local copies, waits for them, and re-layouts  11.3 us (8%)
  other arithmetic  2.09 us (1%)
    all_to_all x1, blocking collectives, on_device(): lax.all_to_all(sent, AXES, split_axis=0, concat_axis=0, tiled=True, axis_...  26.5 us
    pallas_call x4, Pallas kernels, call(): pl.pallas_call(kernel, out_shape=[jax.ShapeDtypeStruct(s, jnp.float32) fo...  25.5 us
    ppermute x1, starting transfers between devices, on_device(): hi = lax.ppermute(minus, AXES, hop(-1, 0))  14.6 us
    ppermute x1, waiting for transfers between devices, on_device(): lo = lax.ppermute(plus, AXES, hop(1, 1))  12.1 us
    ppermute x1, waiting for transfers between devices, on_device(): hi = lax.ppermute(minus, AXES, hop(-1, 0))  7.97 us
    ppermute x1, waiting for transfers between devices, on_device(): lo = lax.ppermute(plus, AXES, hop(1, 0))  5.61 us
    ppermute x1, waiting for transfers between devices, on_device(): hi = lax.ppermute(minus, AXES, hop(-1, 1))  5.5 us
    unnamed x21, local copies, waits for them, and re-layouts  5.04 us
  transfers between devices with their start and end apart: 5, of which 4 were waited for; matrix products, arithmetic and copies ran while one was open for 4% of the time, Pallas kernels for 0%

profile of v1, /device:TPU:24, one launch (start us, length us, event | category | flops | bytes accessed | tf_op | source)
XLA Modules:
  0.0 146.5 jit_solution(17159034978568819301)
XLA Ops:
  0.0 0.7 constant_dynamic-slice_fusion.1
  0.7 0.8 dynamic-slice.1
  1.5 0.6 select_maximum_fusion.1.extra_ref
  2.1 5.3 %shard_map.91 = f32[8,408,128]{2,1,0:T(8,128)} custom-call(f32[768,512]{1,0:T(8,128)} %bitcast.16, f32[512,512]{1,0:T(8,128)} %z_ref.1, f32[24,128]{1,0:T(8,128)} %select_maximum_fusion.1.extra_ref), custom_call_target="tpu_custom_call" | custom-call | tf_op jit(solution)/shard_map/pallas_call | solution.py:174
  7.4 0.0 copy-start.4
  7.4 0.0 copy-start.5
  7.4 0.0 copy-start.6
  7.4 0.0 copy-start.7
  7.4 4.4 %all-to-all-start = ((f32[8,408,128]{2,1,0:T(8,128)}), f32[8,408,128]{2,1,0:T(8,128)S(1)}, u32[]{:S(2)}, u32[]{:S(2)}) async-start(f32[8,408,128]{2,1,0:T(8,128)} %shard_map.91), calls=%async_computation | async-start | bytes 3342336 | tf_op jit(solution)/shard_map/all_to_all | solution.py:219
  11.9 0.0 copy-done.4
  11.9 0.0 copy-done.5
  11.9 0.0 copy-done.6
  11.9 0.0 copy-done.7
  11.9 0.6 fusion.3
  19.8 0.7 fusion.4
  35.4 0.0 all-to-all-done
  35.4 0.1 slice.89.own
  35.5 0.0 copy-start
  35.6 0.8 dynamic-slice_dynamic-update-slice_fusion.5
  36.4 0.8 dynamic-slice_dynamic-update-slice_fusion.4
  37.2 0.8 dynamic-slice_dynamic-update-slice_fusion.3
  38.0 0.8 dynamic-slice_dynamic-update-slice_fusion.2
  38.8 0.8 dynamic-slice_dynamic-update-slice_fusion.1
  39.6 0.0 copy-done
  39.6 0.8 dynamic-slice_dynamic-update-slice_fusion
  40.4 14.6 %collective-permute-start.1 = (f32[6,384,128]{2,1,0:T(8,128)}, f32[6,384,128]{2,1,0:T(8,128)S(1)}, u32[]{:S(2)}, u32[]{:S(2)}) collective-permute-start(f32[6,384,128]{2,1,0:T(8,128)} %get-tuple-element.11), channel_id=1, source_target_pairs={{0,44},{1,673},{2,46},{3,675},{4,0},{5,677},{6,2},{7,679},{8,4},{9... | collective-permute-start | bytes 3538952 | tf_op jit(solution)/shard_map/ppermute | solution.py:235
  55.0 1.9 %collective-permute-start = (f32[6,384,128]{2,1,0:T(8,128)}, f32[6,384,128]{2,1,0:T(8,128)}, u32[]{:S(2)}, u32[]{:S(2)}) collective-permute-start(f32[6,384,128]{2,1,0:T(8,128)} %get-tuple-element.12), channel_id=1, source_target_pairs={{0,4},{1,97},{2,6},{3,99},{4,8},{5,101},{6,10},{7,103},{8,12},{9,1... | collective-permute-start | bytes 3538952 | tf_op jit(solution)/shard_map/ppermute | solution.py:234
  56.9 0.8 dynamic-slice.2
  57.8 0.8 constant_dynamic-slice_fusion
  58.5 0.9 constant_dynamic-slice_fusion.2
  59.5 0.7 fusion.2.ym
  60.3 0.7 select_maximum_fusion.xm
  61.0 8.0 %collective-permute-done.1.hi = f32[6,384,128]{2,1,0:T(8,128)S(1)} collective-permute-done((f32[6,384,128]{2,1,0:T(8,128)}, f32[6,384,128]{2,1,0:T(8,128)S(1)}, u32[]{:S(2)}, u32[]{:S(2)}) %collective-permute-start.1) | collective-permute-done | bytes 1179680 | tf_op jit(solution)/shard_map/ppermute | solution.py:235
  69.0 0.0 copy-start.1
  69.0 5.6 %collective-permute-done.lo = f32[6,384,128]{2,1,0:T(8,128)} collective-permute-done((f32[6,384,128]{2,1,0:T(8,128)}, f32[6,384,128]{2,1,0:T(8,128)}, u32[]{:S(2)}, u32[]{:S(2)}) %collective-permute-start) | collective-permute-done | bytes 1179680 | tf_op jit(solution)/shard_map/ppermute | solution.py:234
  74.6 0.0 copy-done.1
  74.6 10.3 %shard_map.92 = (f32[8,384,128]{2,1,0:T(8,128)}, f32[6,384,128]{2,1,0:T(8,128)}, f32[6,384,128]{2,1,0:T(8,128)}) custom-call(s32[1]{0:T(128)} %bitcast.core_ref, f32[8,384,128]{2,1,0:T(8,128)} %copy-done, f32[6,384,128]{2,1,0:T(8,128)} %collective-permute-done.lo, f32[6,384,128]{2,1,0:T(8,128)} %copy-done.1, f32[64,160]{1,0:T(8,128)} %fusion.2.ym, ...), custom_call_target="tpu_custom_call" | custom-call | tf_op jit(solution)/shard_map/pallas_call | solution.py:174
  84.9 4.7 %collective-permute-start.2 = (f32[6,384,128]{2,1,0:T(8,128)}, f32[6,384,128]{2,1,0:T(8,128)S(1)}, u32[]{:S(2)}, u32[]{:S(2)}) collective-permute-start(f32[6,384,128]{2,1,0:T(8,128)} %get-tuple-element.9), channel_id=1, source_target_pairs={{0,96},{1,5},{2,98},{3,7},{4,100},{5,9},{6,102},{7,11},{8,104},{9,... | collective-permute-start | bytes 3538952 | tf_op jit(solution)/shard_map/ppermute | solution.py:242
  89.6 1.9 %collective-permute-start.3 = (f32[6,384,128]{2,1,0:T(8,128)}, f32[6,384,128]{2,1,0:T(8,128)S(1)}, u32[]{:S(2)}, u32[]{:S(2)}) collective-permute-start(f32[6,384,128]{2,1,0:T(8,128)} %get-tuple-element.10), channel_id=1, source_target_pairs={{0,672},{1,45},{2,674},{3,47},{4,676},{5,1},{6,678},{7,3},{8,680},... | collective-permute-start | bytes 3538952 | tf_op jit(solution)/shard_map/ppermute | solution.py:243
  91.5 12.1 %collective-permute-done.2.lo = f32[6,384,128]{2,1,0:T(8,128)S(1)} collective-permute-done((f32[6,384,128]{2,1,0:T(8,128)}, f32[6,384,128]{2,1,0:T(8,128)S(1)}, u32[]{:S(2)}, u32[]{:S(2)}) %collective-permute-start.2) | collective-permute-done | bytes 1179680 | tf_op jit(solution)/shard_map/ppermute | solution.py:242
  103.6 0.0 copy-start.2
  103.6 5.5 %collective-permute-done.3.hi = f32[6,384,128]{2,1,0:T(8,128)S(1)} collective-permute-done((f32[6,384,128]{2,1,0:T(8,128)}, f32[6,384,128]{2,1,0:T(8,128)S(1)}, u32[]{:S(2)}, u32[]{:S(2)}) %collective-permute-start.3) | collective-permute-done | bytes 1179680 | tf_op jit(solution)/shard_map/ppermute | solution.py:243
  109.1 0.0 copy-start.3
  109.1 0.0 copy-done.2
  109.1 1.0 copy-done.3
  110.1 6.4 %shard_map.93 = f32[8,384,128]{2,1,0:T(8,128)} custom-call(s32[1]{0:T(128)} %bitcast.core_ref, f32[8,384,128]{2,1,0:T(8,128)} %get-tuple-element.8.own, f32[6,384,128]{2,1,0:T(8,128)} %copy-done.2, f32[6,384,128]{2,1,0:T(8,128)} %copy-done.3, f32[64,160]{1,0:T(8,128)} %fusion.2.ym, f32[96,192]{1,0:T(8,128)} %select_maximum_fusion.xm), custom_call_target="tpu_custom_call" | custom-call | tf_op jit(solution)/shard_map/pallas_call | solution.py:174
  116.5 26.5 %all_to_all.10.got = f32[8,384,128]{2,1,0:T(8,128)} all-to-all(f32[8,384,128]{2,1,0:T(8,128)} %shard_map.93), channel_id=1, replica_groups={{0,1,2,3,48,49,50,51},{4,5,6,7,52,53,54,55},{8,9,10,11,56,57,58,59},{12..., dimensions={0} | all-to-all | bytes 3145728 | tf_op jit(solution)/shard_map/all_to_all | solution.py:245
  143.0 3.5 %shard_map.94 = f32[768,512]{1,0:T(8,128)} custom-call(f32[8,384,128]{2,1,0:T(8,128)} %all_to_all.10.got, f32[768,512]{1,0:T(8,128)} %bitcast.17), custom_call_target="tpu_custom_call" | custom-call | tf_op jit(solution)/shard_map/pallas_call | solution.py:174
  (6 shorter events, 0.0 us)
Async XLA Ops:
  7.4 4.5 %copy-start.4 = (s32[6]{0:T(128)S(1)}, s32[6]{0:T(128)}, u32[]{:S(2)}) copy-start(s32[6]{0:T(128)} %constant.63.clone) | copy-start | bytes 76
  7.4 4.5 %copy-start.5 = (s32[6]{0:T(128)S(1)}, s32[6]{0:T(128)}, u32[]{:S(2)}) copy-start(s32[6]{0:T(128)} %constant.62.clone) | copy-start | bytes 76
  7.4 4.5 %copy-start.6 = (s32[6]{0:T(128)S(1)}, s32[6]{0:T(128)}, u32[]{:S(2)}) copy-start(s32[6]{0:T(128)} %constant.61.clone) | copy-start | bytes 76
  7.4 4.5 %copy-start.7 = (s32[6]{0:T(128)S(1)}, s32[6]{0:T(128)}, u32[]{:S(2)}) copy-start(s32[6]{0:T(128)} %constant.60.clone) | copy-start | bytes 76
  7.4 28.0 %all-to-all-start = ((f32[8,408,128]{2,1,0:T(8,128)}), f32[8,408,128]{2,1,0:T(8,128)S(1)}, u32[]{:S(2)}, u32[]{:S(2)}) async-start(f32[8,408,128]{2,1,0:T(8,128)} %shard_map.91), calls=%async_computation | async-start | bytes 3342336 | tf_op jit(solution)/shard_map/all_to_all | solution.py:219
  35.5 4.0 %copy-start = (f32[8,384,128]{2,1,0:T(8,128)}, f32[8,384,128]{2,1,0:T(8,128)S(1)}, u32[]{:S(2)}) copy-start(f32[8,384,128]{2,1,0:T(8,128)S(1)} %slice.89.own) | copy-start | bytes 4718596
  40.4 28.6 %collective-permute-start.1 = (f32[6,384,128]{2,1,0:T(8,128)}, f32[6,384,128]{2,1,0:T(8,128)S(1)}, u32[]{:S(2)}, u32[]{:S(2)}) collective-permute-start(f32[6,384,128]{2,1,0:T(8,128)} %get-tuple-element.11), channel_id=1, source_target_pairs={{0,44},{1,673},{2,46},{3,675},{4,0},{5,677},{6,2},{7,679},{8,4},{9... | collective-permute-start | bytes 3538952 | tf_op jit(solution)/shard_map/ppermute | solution.py:235
  55.0 19.6 %collective-permute-start = (f32[6,384,128]{2,1,0:T(8,128)}, f32[6,384,128]{2,1,0:T(8,128)}, u32[]{:S(2)}, u32[]{:S(2)}) collective-permute-start(f32[6,384,128]{2,1,0:T(8,128)} %get-tuple-element.12), channel_id=1, source_target_pairs={{0,4},{1,97},{2,6},{3,99},{4,8},{5,101},{6,10},{7,103},{8,12},{9,1... | collective-permute-start | bytes 3538952 | tf_op jit(solution)/shard_map/ppermute | solution.py:234
  69.0 5.6 %copy-start.1 = (f32[6,384,128]{2,1,0:T(8,128)}, f32[6,384,128]{2,1,0:T(8,128)S(1)}, u32[]{:S(2)}) copy-start(f32[6,384,128]{2,1,0:T(8,128)S(1)} %collective-permute-done.1.hi) | copy-start | bytes 3538948
  84.9 18.7 %collective-permute-start.2 = (f32[6,384,128]{2,1,0:T(8,128)}, f32[6,384,128]{2,1,0:T(8,128)S(1)}, u32[]{:S(2)}, u32[]{:S(2)}) collective-permute-start(f32[6,384,128]{2,1,0:T(8,128)} %get-tuple-element.9), channel_id=1, source_target_pairs={{0,96},{1,5},{2,98},{3,7},{4,100},{5,9},{6,102},{7,11},{8,104},{9,... | collective-permute-start | bytes 3538952 | tf_op jit(solution)/shard_map/ppermute | solution.py:242
  89.6 19.5 %collective-permute-start.3 = (f32[6,384,128]{2,1,0:T(8,128)}, f32[6,384,128]{2,1,0:T(8,128)S(1)}, u32[]{:S(2)}, u32[]{:S(2)}) collective-permute-start(f32[6,384,128]{2,1,0:T(8,128)} %get-tuple-element.10), channel_id=1, source_target_pairs={{0,672},{1,45},{2,674},{3,47},{4,676},{5,1},{6,678},{7,3},{8,680},... | collective-permute-start | bytes 3538952 | tf_op jit(solution)/shard_map/ppermute | solution.py:243
  103.6 5.5 %copy-start.2 = (f32[6,384,128]{2,1,0:T(8,128)}, f32[6,384,128]{2,1,0:T(8,128)S(1)}, u32[]{:S(2)}) copy-start(f32[6,384,128]{2,1,0:T(8,128)S(1)} %collective-permute-done.2.lo) | copy-start | bytes 3538948
  109.1 1.0 copy-start.3

commit v2 on v1

--- a/solution.py
+++ b/solution.py
@@ -11,6 +11,9 @@
 ROWS = 384
 EXTRA = 24
 INTERPRET = False
+Y_UNROLL = 2
+X_UNROLL = 2
+VMEM_LIMIT = 24 * 2**20
 
 
 def split(v):
@@ -24,17 +27,40 @@
     return mul(ah, bh) + (mul(ah, bl) + mul(al, bh))
 
 
+def stack(m):
+    return jnp.concatenate(split(m), axis=0)
+
+
+def factor_dot(m, cols):
+    n = m.shape[0] // 2
+    ch, cl = split(cols)
+    mul = lambda p, q: lax.dot_general(p, q, (((1,), (0,)), ((), ())), preferred_element_type=jnp.float32)
+    both = mul(m, ch)
+    return both[:n] + (both[n:] + mul(m[:n], cl))
+
+
 def halves(a, b, low):
     return jnp.where(low, a, pltpu.roll(b, 64, 1)), jnp.where(low, pltpu.roll(a, 64, 1), b)
 
 
+def core_of():
+    return lax.rem(lax.axis_index("grp"), 2)
+
+
 def low_lanes(rows):
     return lax.broadcasted_iota(jnp.int32, (rows, 128), 1) < 64
 
 
-def depth_kernel(field_ref, z_ref, extra_ref, out_ref):
-    for d in range(8):
-        out_ref[d, pl.ds(ROWS, EXTRA), :] = extra_ref[...]
+def depth_kernel(field_ref, z_ref, panel_ref, out_ref):
+    share = lax.rem(lax.axis_index("grp"), 4)
+    for s in range(4):
+        @pl.when(share == s)
+        def _():
+            rows = panel_ref[pl.ds(12 * s, 12), :]
+            for d in range(8):
+                out_ref[d, pl.ds(ROWS, 12), :] = rows[:, :128]
+                out_ref[d, pl.ds(ROWS + 12, 12), pl.ds(0, 16)] = rows[:, 128:]
+
     for u in range(2):
         zs = split(z_ref[pl.ds(256 * u, 256), :])
         for m in range(4):
@@ -56,50 +82,68 @@
 
 
 def y_pass(own, up, down, ym, emit):
-    ys = split(ym[...])
+    ys = stack(ym[...])
     for xh in range(2):
         def step(i, carry):
-            cols = []
-            for j in range(2):
-                at = pl.ds(pl.multiple_of((2 * i + j) * 16, 16), 16)
-                cols.append(
-                    jnp.concatenate(
-                        [up[3 * xh + s, at, :] for s in range(3)]
-                        + [own[4 * xh + s, at, :] for s in range(4)]
-                        + [down[3 * xh + s, at, :] for s in range(3)],
-                        axis=0,
+            for k in range(Y_UNROLL):
+                cols = []
+                for j in range(2):
+                    at = pl.ds(pl.multiple_of((2 * (Y_UNROLL * i + k) + j) * 16, 16), 16)
+                    cols.append(
+                        jnp.concatenate(
+                            [up[3 * xh + s, at, :] for s in range(3)]
+                            + [own[4 * xh + s, at, :] for s in range(4)]
+                            + [down[3 * xh + s, at, :] for s in range(3)],
+                            axis=0,
+                        )
                     )
-                )
-            r = dot3(ys, split(jnp.concatenate(cols, axis=1)), ((1,), (0,)))
-            for j in range(2):
-                emit(xh, 2 * i + j, r[:, 128 * j : 128 * j + 128])
+                r = factor_dot(ys, jnp.concatenate(cols, axis=1))
+                for j in range(2):
+                    emit(xh, 2 * (Y_UNROLL * i + k) + j, r[:, 128 * j : 128 * j + 128])
             return carry
 
-        lax.fori_loop(0, 12, step, 0)
+        lax.fori_loop(0, 12 // Y_UNROLL, step, 0)
 
 
 def x_pass(own, left, right, xm, emit):
-    xs = split(xm[...])
+    xs = stack(xm[...])
     for s in range(4):
         def step(i, carry):
-            cols = []
-            for j in range(2):
-                at = pl.ds(pl.multiple_of((2 * i + j) * 48, 16), 48)
-                cols.append(
-                    jnp.concatenate(
-                        [left[s, at, :], own[s, at, :], own[4 + s, at, :], right[s, at, :]], axis=0
+            for k in range(X_UNROLL):
+                cols = []
+                for j in range(2):
+                    at = pl.ds(pl.multiple_of((2 * (X_UNROLL * i + k) + j) * 48, 16), 48)
+                    cols.append(
+                        jnp.concatenate(
+                            [left[s, at, :], own[s, at, :], own[4 + s, at, :], right[s, at, :]], axis=0
+                        )
                     )
-                )
-            r = dot3(xs, split(jnp.concatenate(cols, axis=1)), ((1,), (0,)))
-            for j in range(2):
-                emit(s, 2 * i + j, r[:, 128 * j : 128 * j + 128])
+                r = factor_dot(xs, jnp.concatenate(cols, axis=1))
+                for j in range(2):
+                    emit(s, 2 * (X_UNROLL * i + k) + j, r[:, 128 * j : 128 * j + 128])
             return carry
 
-        lax.fori_loop(0, 4, step, 0)
-
-
-def first_kernel(core_ref, own, lo, hi, ym, xm, out, plus, minus):
-    core = core_ref[0]
+        lax.fori_loop(0, 4 // X_UNROLL, step, 0)
+
+
+def pick_kernel(own, plus, minus):
+    core = core_of()
+
+    @pl.when(core == 0)
+    def _():
+        for i, (p, m) in enumerate(((1, 0), (2, 1), (3, 2), (5, 4), (6, 5), (7, 6))):
+            plus[i] = own[p, pl.ds(0, ROWS), :]
+            minus[i] = own[m, pl.ds(0, ROWS), :]
+
+    @pl.when(core == 1)
+    def _():
+        for s in range(4):
+            plus[s] = own[4 + s, pl.ds(0, ROWS), :]
+            minus[s] = own[s, pl.ds(0, ROWS), :]
+
+
+def first_kernel(own, lo, hi, ym, xm, out, plus, minus):
+    core = core_of()
 
     @pl.when(core == 0)
     def _():
@@ -130,8 +174,8 @@
                 minus[3 * xh + s] = out[4 * xh + s]
 
 
-def second_kernel(core_ref, own, lo, hi, ym, xm, out):
-    core = core_ref[0]
+def second_kernel(own, lo, hi, ym, xm, out):
+    core = core_of()
 
     @pl.when(core == 0)
     def _():
@@ -167,15 +211,19 @@
                     out_ref[at, lanes] = r * scale_ref[at, lanes]
 
 
-def call(kernel, shapes, *args, scalar=False):
+def call(kernel, shapes, *args, plain=False):
     specs = [pl.BlockSpec(memory_space=pltpu.VMEM) for _ in args]
-    if scalar:
-        specs[0] = pl.BlockSpec(memory_space=pltpu.SMEM)
+    outs = [jax.ShapeDtypeStruct(s, jnp.float32) for s in shapes]
+    if not INTERPRET:
+        args = [pltpu.with_memory_space_constraint(a, pltpu.VMEM) for a in args]
+        if not plain:
+            outs = [pltpu.VMEM(s, jnp.float32) for s in shapes]
     return pl.pallas_call(
         kernel,
-        out_shape=[jax.ShapeDtypeStruct(s, jnp.float32) for s in shapes],
+        out_shape=outs,
         in_specs=specs,
         out_specs=[pl.BlockSpec(memory_space=pltpu.VMEM) for _ in shapes],
+        compiler_params=pltpu.CompilerParams(vmem_limit_bytes=VMEM_LIMIT),
         interpret=INTERPRET,
     )(*args)
 
@@ -205,17 +253,14 @@
 
 def on_device(eights, hop, field, x_panel, y_factor, z_factor, scaling):
     grp = lax.axis_index("grp")
-    core = grp % 2
-    slab, share = grp // 4, grp % 4
+    slab = grp // 4
     ny = y_factor.shape[0]
 
-    quarter = lax.dynamic_slice_in_dim(x_panel, 12 * share, 12, 0)
-    extra = jnp.concatenate([quarter[:, :128], jnp.pad(quarter[:, 128:], ((0, 0), (0, 112)))], axis=0)
     band = lax.dynamic_slice_in_dim(y_factor, 64 * slab, 64, 0)
     band = jnp.concatenate([band[:, ny - 48 :], band, band[:, :64]], axis=1)
     ym = lax.dynamic_slice_in_dim(band, 64 * slab, 160, 1)
 
-    (sent,) = call(depth_kernel, [(8, ROWS + EXTRA, 128)], field.reshape(768, 512), z_factor, extra)
+    (sent,) = call(depth_kernel, [(8, ROWS + EXTRA, 128)], field.reshape(768, 512), z_factor, x_panel, plain=True)
     got = lax.all_to_all(sent, AXES, split_axis=0, concat_axis=0, tiled=True, axis_index_groups=eights)
 
     tail = got[:, ROWS:, :]
@@ -223,27 +268,19 @@
     xm = jnp.concatenate(
         [jnp.pad(panel[0], ((0, 0), (0, 48))), jnp.pad(panel[1], ((0, 0), (48, 0)))], axis=0
     )
-    own = got[:, :ROWS, :]
-
-    def pick(first, second):
-        at = jnp.where(core == 0, jnp.array(first), jnp.array(second))
-        return jnp.concatenate([lax.dynamic_slice_in_dim(own, at[i], 1, 0) for i in range(6)], axis=0)
-
-    plus = pick((1, 2, 3, 5, 6, 7), (4, 5, 6, 7, 7, 7))
-    minus = pick((0, 1, 2, 4, 5, 6), (0, 1, 2, 3, 3, 3))
+    plus, minus = call(pick_kernel, [(6, ROWS, 128), (6, ROWS, 128)], got)
     lo = lax.ppermute(plus, AXES, hop(1, 0))
     hi = lax.ppermute(minus, AXES, hop(-1, 0))
-    flag = core.astype(jnp.int32).reshape(1)
     own, plus, minus = call(
         first_kernel,
         [(8, ROWS, 128), (6, ROWS, 128), (6, ROWS, 128)],
-        flag, own, lo, hi, ym, xm, scalar=True,
+        got, lo, hi, ym, xm,
     )
     lo = lax.ppermute(plus, AXES, hop(1, 1))
     hi = lax.ppermute(minus, AXES, hop(-1, 1))
-    (sent,) = call(second_kernel, [(8, ROWS, 128)], flag, own, lo, hi, ym, xm, scalar=True)
+    (sent,) = call(second_kernel, [(8, ROWS, 128)], own, lo, hi, ym, xm)
     got = lax.all_to_all(sent, AXES, split_axis=0, concat_axis=0, tiled=True, axis_index_groups=eights)
-    (out,) = call(last_kernel, [(768, 512)], got, scaling.reshape(768, 512))
+    (out,) = call(last_kernel, [(768, 512)], got, scaling.reshape(768, 512), plain=True)
     return out.reshape(16, 48, 512)
 
 

time: 147 us -> 122 us (0.83)
  blocking collectives: 26.5 us -> 50.9 us
  between operations: 22.4 us -> 0.16 us
  Pallas kernels: 25.5 us -> 12.3 us
  local copies, waits for them, and re-layouts: 11.3 us -> 6.01 us
  starting transfers between devices: 27.5 us -> 23.1 us
  waiting for transfers between devices: 31.2 us -> 28.5 us
  other arithmetic: 2.09 us -> 0.21 us
    all_to_all x1 -> x2, blocking collectives: 26.5 us -> 50.9 us  [on_device(): lax.all_to_all(sent, AXES, split_axis=0, concat_axis=0, tiled=True, axis_...]
    pallas_call x4 -> x5, Pallas kernels: 25.5 us -> 12.3 us  [call(): pl.pallas_call(kernel, out_shape=outs, in_specs=specs, out_specs=[pl.Bloc...]
    ppermute x1, waiting for transfers between devices: 7.97 us -> 1.57 us  [on_device(): hi = lax.ppermute(minus, AXES, hop(-1, 0))]
    all_to_all x1 -> x0, starting transfers between devices: 4.45 us -> none  [on_device(): lax.all_to_all(sent, AXES, split_axis=0, concat_axis=0, tiled=True, axis_...]
    ppermute x1, waiting for transfers between devices: 5.61 us -> 9.57 us  [on_device(): lo = lax.ppermute(plus, AXES, hop(1, 0))]
    slice x5 -> x0, local copies, waits for them, and re-layouts: 2.9 us -> none  [the longest x2 1.3 us: pick(): at[i]]
    ppermute x1, starting transfers between devices: 1.92 us -> 4.27 us  [on_device(): lo = lax.ppermute(plus, AXES, hop(1, 0))]
    ppermute x1, starting transfers between devices: 14.6 us -> 12.2 us  [on_device(): hi = lax.ppermute(minus, AXES, hop(-1, 0))]
  transfers between devices with their start and end apart: 5 -> 4, of which waited for: 4 -> 4; matrix products, arithmetic and copies ran while one was open for 4% -> 2% of each run, Pallas kernels for 0% -> 0%
where the time goes in v2:
time: 122 us; the launch traced here: 121 us
  blocking collectives  50.9 us (42%)
  waiting for transfers between devices  28.5 us (23%)
  starting transfers between devices  23.1 us (19%)
  Pallas kernels  12.3 us (10%)
  local copies, waits for them, and re-layouts  6.01 us (5%)
    all_to_all x2, blocking collectives, on_device(): lax.all_to_all(sent, AXES, split_axis=0, concat_axis=0, tiled=True, axis_...  50.9 us
    pallas_call x5, Pallas kernels, call(): pl.pallas_call(kernel, out_shape=outs, in_specs=specs, out_specs=[pl.Bloc...  12.3 us
    ppermute x1, starting transfers between devices, on_device(): hi = lax.ppermute(minus, AXES, hop(-1, 0))  12.2 us
    ppermute x1, waiting for transfers between devices, on_device(): lo = lax.ppermute(plus, AXES, hop(1, 1))  11.8 us
    ppermute x1, waiting for transfers between devices, on_device(): lo = lax.ppermute(plus, AXES, hop(1, 0))  9.57 us
    ppermute x1, waiting for transfers between devices, on_device(): hi = lax.ppermute(minus, AXES, hop(-1, 1))  5.61 us
    ppermute x1, starting transfers between devices, on_device(): lo = lax.ppermute(plus, AXES, hop(1, 1))  4.69 us
    ppermute x1, starting transfers between devices, on_device(): lo = lax.ppermute(plus, AXES, hop(1, 0))  4.27 us
  transfers between devices with their start and end apart: 4, of which 4 were waited for; matrix products, arithmetic and copies ran while one was open for 2% of the time, Pallas kernels for 0%

profile of v2, /device:TPU:24, one launch (start us, length us, event | category | flops | bytes accessed | tf_op | source)
XLA Modules:
  0.0 121.2 jit_solution(10893139360075841713)
XLA Ops:
  0.0 0.0 copy-start
  0.0 1.4 %copy-done = f32[16,48,512]{2,1,0:T(8,128)S(1)} copy-done((f32[16,48,512]{2,1,0:T(8,128)S(1)}, f32[16,48,512]{2,1,0:T(8,128)}, u32[]{:S(2)}) %copy-start) | copy-done | bytes 1572888
  1.4 0.0 copy-start.2
  1.4 1.2 %copy-done.2 = f32[512,512]{1,0:T(8,128)S(1)} copy-done((f32[512,512]{1,0:T(8,128)S(1)}, f32[512,512]{1,0:T(8,128)}, u32[]{:S(2)}) %copy-start.2) | copy-done | bytes 1048600
  2.6 0.0 copy-start.3
  2.6 0.8 copy-done.3
  3.4 2.4 %shard_map.55 = f32[8,408,128]{2,1,0:T(8,128)S(1)} custom-call(f32[768,512]{1,0:T(8,128)S(1)} %bitcast.3, f32[512,512]{1,0:T(8,128)S(1)} %copy-done.2, f32[48,144]{1,0:T(8,128)S(1)} %copy-done.3), custom_call_target="tpu_custom_call" | custom-call | tf_op jit(solution)/shard_map/pallas_call | solution.py:221
  5.8 26.7 %all_to_all.10.own = f32[8,408,128]{2,1,0:T(8,128)S(1)} all-to-all(f32[8,408,128]{2,1,0:T(8,128)S(1)} %shard_map.55), channel_id=1, replica_groups={{0,1,2,3,48,49,50,51},{4,5,6,7,52,53,54,55},{8,9,10,11,56,57,58,59},{12..., dimensions={0} | all-to-all | bytes 3342336 | tf_op jit(solution)/shard_map/all_to_all | solution.py:264
  32.5 1.6 %shard_map.56 = (f32[6,384,128]{2,1,0:T(8,128)}, f32[6,384,128]{2,1,0:T(8,128)}) custom-call(f32[8,408,128]{2,1,0:T(8,128)S(1)} %all_to_all.10.own), custom_call_target="tpu_custom_call" | custom-call | tf_op jit(solution)/shard_map/pallas_call | solution.py:221
  34.1 4.3 %collective-permute-start = (f32[6,384,128]{2,1,0:T(8,128)}, f32[6,384,128]{2,1,0:T(8,128)S(1)}, u32[]{:S(2)}, u32[]{:S(2)}) collective-permute-start(f32[6,384,128]{2,1,0:T(8,128)} %get-tuple-element.10), channel_id=1, source_target_pairs={{0,4},{1,97},{2,6},{3,99},{4,8},{5,101},{6,10},{7,103},{8,12},{9,1... | collective-permute-start | bytes 3538952 | tf_op jit(solution)/shard_map/ppermute | solution.py:272
  38.4 12.2 %collective-permute-start.1 = (f32[6,384,128]{2,1,0:T(8,128)}, f32[6,384,128]{2,1,0:T(8,128)}, u32[]{:S(2)}, u32[]{:S(2)}) collective-permute-start(f32[6,384,128]{2,1,0:T(8,128)} %get-tuple-element.11), channel_id=1, source_target_pairs={{0,44},{1,673},{2,46},{3,675},{4,0},{5,677},{6,2},{7,679},{8,4},{9... | collective-permute-start | bytes 3538952 | tf_op jit(solution)/shard_map/ppermute | solution.py:273
  50.7 0.8 dynamic-slice
  51.5 0.8 constant_dynamic-slice_fusion
  52.3 0.9 constant_dynamic-slice_fusion.1
  53.2 0.1 fusion.2.ym
  53.4 0.1 select_maximum_fusion.xm
  53.5 9.6 %collective-permute-done.lo = f32[6,384,128]{2,1,0:T(8,128)S(1)} collective-permute-done((f32[6,384,128]{2,1,0:T(8,128)}, f32[6,384,128]{2,1,0:T(8,128)S(1)}, u32[]{:S(2)}, u32[]{:S(2)}) %collective-permute-start) | collective-permute-done | bytes 1179680 | tf_op jit(solution)/shard_map/ppermute | solution.py:272
  63.1 1.6 %collective-permute-done.1.hi = f32[6,384,128]{2,1,0:T(8,128)} collective-permute-done((f32[6,384,128]{2,1,0:T(8,128)}, f32[6,384,128]{2,1,0:T(8,128)}, u32[]{:S(2)}, u32[]{:S(2)}) %collective-permute-start.1) | collective-permute-done | bytes 1179680 | tf_op jit(solution)/shard_map/ppermute | solution.py:273
  64.6 4.9 %shard_map.57 = (f32[8,384,128]{2,1,0:T(8,128)S(1)}, f32[6,384,128]{2,1,0:T(8,128)S(1)}, f32[6,384,128]{2,1,0:T(8,128)S(1)}) custom-call(f32[8,408,128]{2,1,0:T(8,128)S(1)} %all_to_all.10.own, f32[6,384,128]{2,1,0:T(8,128)S(1)} %collective-permute-done.lo, f32[6,384,128]{2,1,0:T(8,128)} %collective-permute-done.1.hi, f32[64,160]{1,0:T(8,128)S(1)} %fusion.2.ym, ...), custom_call_target="tpu_custom_call" | custom-call | tf_op jit(solution)/shard_map/pallas_call | solution.py:221
  69.5 4.7 %collective-permute-start.2 = (f32[6,384,128]{2,1,0:T(8,128)S(1)}, f32[6,384,128]{2,1,0:T(8,128)S(1)}, u32[]{:S(2)}, u32[]{:S(2)}) collective-permute-start(f32[6,384,128]{2,1,0:T(8,128)S(1)} %get-tuple-element.13), channel_id=1, source_target_pairs={{0,96},{1,5},{2,98},{3,7},{4,100},{5,9},{6,102},{7,11},{8,104},{9,... | collective-permute-start | bytes 3538952 | tf_op jit(solution)/shard_map/ppermute | solution.py:279
  74.2 1.9 %collective-permute-start.3 = (f32[6,384,128]{2,1,0:T(8,128)S(1)}, f32[6,384,128]{2,1,0:T(8,128)S(1)}, u32[]{:S(2)}, u32[]{:S(2)}) collective-permute-start(f32[6,384,128]{2,1,0:T(8,128)S(1)} %get-tuple-element.14), channel_id=1, source_target_pairs={{0,672},{1,45},{2,674},{3,47},{4,676},{5,1},{6,678},{7,3},{8,680},... | collective-permute-start | bytes 3538952 | tf_op jit(solution)/shard_map/ppermute | solution.py:280
  76.2 11.8 %collective-permute-done.2.lo = f32[6,384,128]{2,1,0:T(8,128)S(1)} collective-permute-done((f32[6,384,128]{2,1,0:T(8,128)S(1)}, f32[6,384,128]{2,1,0:T(8,128)S(1)}, u32[]{:S(2)}, u32[]{:S(2)}) %collective-permute-start.2) | collective-permute-done | bytes 1179680 | tf_op jit(solution)/shard_map/ppermute | solution.py:279
  87.9 5.6 %collective-permute-done.3.hi = f32[6,384,128]{2,1,0:T(8,128)S(1)} collective-permute-done((f32[6,384,128]{2,1,0:T(8,128)S(1)}, f32[6,384,128]{2,1,0:T(8,128)S(1)}, u32[]{:S(2)}, u32[]{:S(2)}) %collective-permute-start.3) | collective-permute-done | bytes 1179680 | tf_op jit(solution)/shard_map/ppermute | solution.py:280
  93.5 1.9 %shard_map.58 = f32[8,384,128]{2,1,0:T(8,128)S(1)} custom-call(f32[8,384,128]{2,1,0:T(8,128)S(1)} %get-tuple-element.12.own, f32[6,384,128]{2,1,0:T(8,128)S(1)} %collective-permute-done.2.lo, f32[6,384,128]{2,1,0:T(8,128)S(1)} %collective-permute-done.3.hi, f32[64,160]{1,0:T(8,128)S(1)} %fusion.2.ym, f32[96,192]{1,0:T(8,128)S(1)} %select_maximum_fusion.xm), custom_call_target="tpu_custom_call" | custom-call | tf_op jit(solution)/shard_map/pallas_call | solution.py:221
  95.4 0.0 copy-start.1
  95.4 24.2 %all_to_all.11.got = f32[8,384,128]{2,1,0:T(8,128)S(1)} all-to-all(f32[8,384,128]{2,1,0:T(8,128)S(1)} %shard_map.58), channel_id=1, replica_groups={{0,1,2,3,48,49,50,51},{4,5,6,7,52,53,54,55},{8,9,10,11,56,57,58,59},{12..., dimensions={0} | all-to-all | bytes 3145728 | tf_op jit(solution)/shard_map/all_to_all | solution.py:282
  119.6 0.0 copy-done.1
  119.6 1.6 %shard_map.59 = f32[768,512]{1,0:T(8,128)} custom-call(f32[8,384,128]{2,1,0:T(8,128)S(1)} %all_to_all.11.got, f32[768,512]{1,0:T(8,128)S(1)} %bitcast.4), custom_call_target="tpu_custom_call" | custom-call | tf_op jit(solution)/shard_map/pallas_call | solution.py:221
  (5 shorter events, 0.0 us)
Async XLA Ops:
  0.0 1.4 %copy-start = (f32[16,48,512]{2,1,0:T(8,128)S(1)}, f32[16,48,512]{2,1,0:T(8,128)}, u32[]{:S(2)}) copy-start(f32[16,48,512]{2,1,0:T(8,128)} %param.5) | copy-start | bytes 4718596
  1.4 1.2 %copy-start.2 = (f32[512,512]{1,0:T(8,128)S(1)}, f32[512,512]{1,0:T(8,128)}, u32[]{:S(2)}) copy-start(f32[512,512]{1,0:T(8,128)} %z_ref.1) | copy-start | bytes 3145732
  2.6 0.8 copy-start.3
  34.1 29.0 %collective-permute-start = (f32[6,384,128]{2,1,0:T(8,128)}, f32[6,384,128]{2,1,0:T(8,128)S(1)}, u32[]{:S(2)}, u32[]{:S(2)}) collective-permute-start(f32[6,384,128]{2,1,0:T(8,128)} %get-tuple-element.10), channel_id=1, source_target_pairs={{0,4},{1,97},{2,6},{3,99},{4,8},{5,101},{6,10},{7,103},{8,12},{9,1... | collective-permute-start | bytes 3538952 | tf_op jit(solution)/shard_map/ppermute | solution.py:272
  38.4 26.3 %collective-permute-start.1 = (f32[6,384,128]{2,1,0:T(8,128)}, f32[6,384,128]{2,1,0:T(8,128)}, u32[]{:S(2)}, u32[]{:S(2)}) collective-permute-start(f32[6,384,128]{2,1,0:T(8,128)} %get-tuple-element.11), channel_id=1, source_target_pairs={{0,44},{1,673},{2,46},{3,675},{4,0},{5,677},{6,2},{7,679},{8,4},{9... | collective-permute-start | bytes 3538952 | tf_op jit(solution)/shard_map/ppermute | solution.py:273
  69.5 18.4 %collective-permute-start.2 = (f32[6,384,128]{2,1,0:T(8,128)S(1)}, f32[6,384,128]{2,1,0:T(8,128)S(1)}, u32[]{:S(2)}, u32[]{:S(2)}) collective-permute-start(f32[6,384,128]{2,1,0:T(8,128)S(1)} %get-tuple-element.13), channel_id=1, source_target_pairs={{0,96},{1,5},{2,98},{3,7},{4,100},{5,9},{6,102},{7,11},{8,104},{9,... | collective-permute-start | bytes 3538952 | tf_op jit(solution)/shard_map/ppermute | solution.py:279
  74.2 19.3 %collective-permute-start.3 = (f32[6,384,128]{2,1,0:T(8,128)S(1)}, f32[6,384,128]{2,1,0:T(8,128)S(1)}, u32[]{:S(2)}, u32[]{:S(2)}) collective-permute-start(f32[6,384,128]{2,1,0:T(8,128)S(1)} %get-tuple-element.14), channel_id=1, source_target_pairs={{0,672},{1,45},{2,674},{3,47},{4,676},{5,1},{6,678},{7,3},{8,680},... | collective-permute-start | bytes 3538952 | tf_op jit(solution)/shard_map/ppermute | solution.py:280
  95.4 24.2 %copy-start.1 = (f32[16,48,512]{2,1,0:T(8,128)S(1)}, f32[16,48,512]{2,1,0:T(8,128)}, u32[]{:S(2)}) copy-start(f32[16,48,512]{2,1,0:T(8,128)} %param.9) | copy-start | bytes 4718596

commit v3 on v2

--- a/solution.py
+++ b/solution.py
@@ -51,21 +51,28 @@
     return lax.broadcasted_iota(jnp.int32, (rows, 128), 1) < 64
 
 
-def depth_kernel(field_ref, z_ref, panel_ref, out_ref):
-    share = lax.rem(lax.axis_index("grp"), 4)
-    for s in range(4):
-        @pl.when(share == s)
-        def _():
-            rows = panel_ref[pl.ds(12 * s, 12), :]
-            for d in range(8):
-                out_ref[d, pl.ds(ROWS, 12), :] = rows[:, :128]
-                out_ref[d, pl.ds(ROWS + 12, 12), pl.ds(0, 16)] = rows[:, 128:]
-
+def depth_kernel(field_hbm, z_hbm, panel_hbm, out_ref, field_ref, z_ref, panel_ref, sems):
+    panel_copy = pltpu.make_async_copy(panel_hbm, panel_ref, sems.at[10])
+    field_copies, z_copies = [], []
     for u in range(2):
+        at = pl.ds(256 * u, 256)
+        z_copies.append(pltpu.make_async_copy(z_hbm.at[at, :], z_ref.at[at, :], sems.at[8 + u]))
+    for m in range(4):
+        for i in range(2):
+            at = pl.ds(48 * (8 * i + 2 * m), 96)
+            field_copies.append(pltpu.make_async_copy(field_hbm.at[at, :], field_ref.at[at, :], sems.at[2 * m + i]))
+    for c in [z_copies[0]] + field_copies + [z_copies[1], panel_copy]:
+        c.start()
+
+    for u in range(2):
+        z_copies[u].wait()
         zs = split(z_ref[pl.ds(256 * u, 256), :])
         for m in range(4):
+            if u == 0 and m % 2 == 0:
+                for c in field_copies[2 * m : 2 * m + 4]:
+                    c.wait()
             ys = (2 * m, 2 * m + 1, 8 + 2 * m, 9 + 2 * m)
-            rows = jnp.concatenate([field_ref[pl.ds(48 * y, 48), :] for y in ys], axis=0)
+            rows = jnp.concatenate([field_ref[pl.ds(96 * m, 96), :], field_ref[pl.ds(384 + 96 * m, 96), :]], axis=0)
             t = dot3(split(rows), zs, ((1,), (1,)))
             for v in range(2):
                 tile = t[:, 128 * v : 128 * v + 128]
@@ -80,9 +87,19 @@
                     o = jnp.where(low_lanes(48), pltpu.roll(a, 64, 1), b)
                     out_ref[d + 1, pl.ds(48 * ys[i], 48), :] = o
 
+    panel_copy.wait()
+    share = lax.rem(lax.axis_index("grp"), 4)
+    for s in range(4):
+        @pl.when(share == s)
+        def _():
+            rows = panel_ref[pl.ds(12 * s, 12), :]
+            for d in range(8):
+                out_ref[d, pl.ds(ROWS, 12), :] = rows[:, :128]
+                out_ref[d, pl.ds(ROWS + 12, 12), pl.ds(0, 16)] = rows[:, 128:]
+
 
 def y_pass(own, up, down, ym, emit):
-    ys = stack(ym[...])
+    ys = stack(ym[:, :160])
     for xh in range(2):
         def step(i, carry):
             for k in range(Y_UNROLL):
@@ -106,7 +123,7 @@
 
 
 def x_pass(own, left, right, xm, emit):
-    xs = stack(xm[...])
+    xs = stack(xm[:, :192])
     for s in range(4):
         def step(i, carry):
             for k in range(X_UNROLL):
@@ -126,9 +143,10 @@
         lax.fori_loop(0, 4 // X_UNROLL, step, 0)
 
 
-def pick_kernel(own, plus, minus):
+def pick_kernel(own, y_ref, plus, minus, ym, xm):
     core = core_of()
-
+    slab = lax.div(lax.axis_index("grp"), 4)
+    ny = y_ref.shape[0]
     @pl.when(core == 0)
     def _():
         for i, (p, m) in enumerate(((1, 0), (2, 1), (3, 2), (5, 4), (6, 5), (7, 6))):
@@ -140,6 +158,16 @@
         for s in range(4):
             plus[s] = own[4 + s, pl.ds(0, ROWS), :]
             minus[s] = own[s, pl.ds(0, ROWS), :]
+
+    few = lax.broadcasted_iota(jnp.int32, (12, 128), 1) < 16
+    for xh in range(2):
+        for s in range(4):
+            p = own[4 * xh + s, pl.ds(ROWS, 12), :]
+            q = jnp.where(few, own[4 * xh + s, pl.ds(ROWS + 12, 12), :], 0.0)
+            w = jnp.concatenate([p, q], axis=1)
+            xm[pl.ds(48 * xh + 12 * s, 12), :] = pltpu.roll(w, 48, 1) if xh else w
+    shift = lax.rem(ny + 48 - 64 * slab, ny)
+    ym[...] = pltpu.roll(y_ref[pl.ds(pl.multiple_of(64 * slab, 64), 64), :], shift, 1)[:, :256]
 
 
 def first_kernel(own, lo, hi, ym, xm, out, plus, minus):
@@ -211,18 +239,19 @@
                     out_ref[at, lanes] = r * scale_ref[at, lanes]
 
 
-def call(kernel, shapes, *args, plain=False):
-    specs = [pl.BlockSpec(memory_space=pltpu.VMEM) for _ in args]
+def call(kernel, shapes, *args, hbm=(), plain=False, scratch=()):
+    vmem = pl.BlockSpec(memory_space=pltpu.VMEM)
     outs = [jax.ShapeDtypeStruct(s, jnp.float32) for s in shapes]
     if not INTERPRET:
-        args = [pltpu.with_memory_space_constraint(a, pltpu.VMEM) for a in args]
+        args = [pltpu.with_memory_space_constraint(a, pltpu.HBM if i in hbm else pltpu.VMEM) for i, a in enumerate(args)]
         if not plain:
             outs = [pltpu.VMEM(s, jnp.float32) for s in shapes]
     return pl.pallas_call(
         kernel,
         out_shape=outs,
-        in_specs=specs,
-        out_specs=[pl.BlockSpec(memory_space=pltpu.VMEM) for _ in shapes],
+        in_specs=[pl.BlockSpec(memory_space=pltpu.HBM) if i in hbm else vmem for i in range(len(args))],
+        out_specs=[vmem for _ in shapes],
+        scratch_shapes=list(scratch),
         compiler_params=pltpu.CompilerParams(vmem_limit_bytes=VMEM_LIMIT),
         interpret=INTERPRET,
     )(*args)
@@ -252,23 +281,21 @@
 
 
 def on_device(eights, hop, field, x_panel, y_factor, z_factor, scaling):
-    grp = lax.axis_index("grp")
-    slab = grp // 4
-    ny = y_factor.shape[0]
-
-    band = lax.dynamic_slice_in_dim(y_factor, 64 * slab, 64, 0)
-    band = jnp.concatenate([band[:, ny - 48 :], band, band[:, :64]], axis=1)
-    ym = lax.dynamic_slice_in_dim(band, 64 * slab, 160, 1)
-
-    (sent,) = call(depth_kernel, [(8, ROWS + EXTRA, 128)], field.reshape(768, 512), z_factor, x_panel, plain=True)
+    (sent,) = call(
+        depth_kernel, [(8, ROWS + EXTRA, 128)], field.reshape(768, 512), z_factor, x_panel,
+        hbm=(0, 1, 2),
+        scratch=[
+            pltpu.VMEM((768, 512), jnp.float32),
+            pltpu.VMEM((512, 512), jnp.float32),
+            pltpu.VMEM((48, 144), jnp.float32),
+            pltpu.SemaphoreType.DMA((11,)),
+        ],
+    )
     got = lax.all_to_all(sent, AXES, split_axis=0, concat_axis=0, tiled=True, axis_index_groups=eights)
 
-    tail = got[:, ROWS:, :]
-    panel = jnp.concatenate([tail[:, :12], tail[:, 12:, :16]], axis=2).reshape(2, 48, 144)
-    xm = jnp.concatenate(
-        [jnp.pad(panel[0], ((0, 0), (0, 48))), jnp.pad(panel[1], ((0, 0), (48, 0)))], axis=0
+    plus, minus, ym, xm = call(
+        pick_kernel, [(6, ROWS, 128), (6, ROWS, 128), (64, 256), (96, 256)], got, y_factor,
     )
-    plus, minus = call(pick_kernel, [(6, ROWS, 128), (6, ROWS, 128)], got)
     lo = lax.ppermute(plus, AXES, hop(1, 0))
     hi = lax.ppermute(minus, AXES, hop(-1, 0))
     own, plus, minus = call(

time: 122 us -> 117 us (0.959)
  local copies, waits for them, and re-layouts: 6.01 us -> 0.01 us
  waiting for transfers between devices: 28.5 us -> 31.1 us
    unnamed x8 -> x4, local copies, waits for them, and re-layouts: 3.44 us -> 0.01 us
    ppermute x1, waiting for transfers between devices: 9.57 us -> 12.2 us  [on_device(): lo = lax.ppermute(plus, AXES, hop(1, 0))]
    slice x4 -> x0, local copies, waits for them, and re-layouts: 1.62 us -> none  [the longest x2 1.6 us: on_device(): band = jnp.concatenate([band[:, ny - 48:], band, band[:, :64]], axis=1)]
  transfers between devices with their start and end apart: 4 -> 4, of which waited for: 4 -> 4; matrix products, arithmetic and copies ran while one was open for 2% -> 0% of each run, Pallas kernels for 0% -> 0%
where the time goes in v3:
time: 117 us
  blocking collectives  51 us (44%)
  waiting for transfers between devices  31.1 us (27%)
  starting transfers between devices  23.1 us (20%)
  Pallas kernels  11.7 us (10%)
    all_to_all x2, blocking collectives, on_device(): lax.all_to_all(sent, AXES, split_axis=0, concat_axis=0, tiled=True, axis_...  51 us
    ppermute x1, waiting for transfers between devices, on_device(): lo = lax.ppermute(plus, AXES, hop(1, 0))  12.2 us
    ppermute x1, starting transfers between devices, on_device(): hi = lax.ppermute(minus, AXES, hop(-1, 0))  12.2 us
    ppermute x1, waiting for transfers between devices, on_device(): lo = lax.ppermute(plus, AXES, hop(1, 1))  11.8 us
    pallas_call x5, Pallas kernels, call(): pl.pallas_call(kernel, out_shape=outs, in_specs=[pl.BlockSpec(memory_spac...  11.7 us
    ppermute x1, waiting for transfers between devices, on_device(): hi = lax.ppermute(minus, AXES, hop(-1, 1))  5.61 us
    ppermute x1, starting transfers between devices, on_device(): lo = lax.ppermute(plus, AXES, hop(1, 1))  4.7 us
    ppermute x1, starting transfers between devices, on_device(): lo = lax.ppermute(plus, AXES, hop(1, 0))  4.28 us
  transfers between devices with their start and end apart: 4, of which 4 were waited for; matrix products, arithmetic and copies ran while one was open for 0% of the time, Pallas kernels for 0%

profile of v3, /device:TPU:24, one launch (start us, length us, event | category | flops | bytes accessed | tf_op | source)
XLA Modules:
  0.0 117.0 jit_solution(7367211561230631304)
XLA Ops:
  0.0 4.2 %shard_map.55 = f32[8,408,128]{2,1,0:T(8,128)S(1)} custom-call(f32[768,512]{1,0:T(8,128)} %bitcast.4, f32[512,512]{1,0:T(8,128)} %z_hbm.1, f32[48,144]{1,0:T(8,128)} %panel_hbm.1), custom_call_target="tpu_custom_call" | custom-call | tf_op jit(solution)/shard_map/pallas_call | solution.py:249
  4.2 0.0 copy-start
  4.3 26.9 %all_to_all.10.own = f32[8,408,128]{2,1,0:T(8,128)S(1)} all-to-all(f32[8,408,128]{2,1,0:T(8,128)S(1)} %shard_map.55), channel_id=1, replica_groups={{0,1,2,3,48,49,50,51},{4,5,6,7,52,53,54,55},{8,9,10,11,56,57,58,59},{12..., dimensions={0} | all-to-all | bytes 3342336 | tf_op jit(solution)/shard_map/all_to_all | solution.py:294
  31.1 0.0 copy-done
  31.1 0.3 shard_map.56
  31.4 4.3 %collective-permute-start = (f32[6,384,128]{2,1,0:T(8,128)S(1)}, f32[6,384,128]{2,1,0:T(8,128)S(1)}, u32[]{:S(2)}, u32[]{:S(2)}) collective-permute-start(f32[6,384,128]{2,1,0:T(8,128)S(1)} %get-tuple-element.12), channel_id=1, source_target_pairs={{0,4},{1,97},{2,6},{3,99},{4,8},{5,101},{6,10},{7,103},{8,12},{9,1... | collective-permute-start | bytes 3538952 | tf_op jit(solution)/shard_map/ppermute | solution.py:299
  35.7 12.2 %collective-permute-start.1 = (f32[6,384,128]{2,1,0:T(8,128)S(1)}, f32[6,384,128]{2,1,0:T(8,128)S(1)}, u32[]{:S(2)}, u32[]{:S(2)}) collective-permute-start(f32[6,384,128]{2,1,0:T(8,128)S(1)} %get-tuple-element.13), channel_id=1, source_target_pairs={{0,44},{1,673},{2,46},{3,675},{4,0},{5,677},{6,2},{7,679},{8,4},{9... | collective-permute-start | bytes 3538952 | tf_op jit(solution)/shard_map/ppermute | solution.py:300
  48.0 12.2 %collective-permute-done.lo = f32[6,384,128]{2,1,0:T(8,128)S(1)} collective-permute-done((f32[6,384,128]{2,1,0:T(8,128)S(1)}, f32[6,384,128]{2,1,0:T(8,128)S(1)}, u32[]{:S(2)}, u32[]{:S(2)}) %collective-permute-start) | collective-permute-done | bytes 1179680 | tf_op jit(solution)/shard_map/ppermute | solution.py:299
  60.2 1.5 %collective-permute-done.1.hi = f32[6,384,128]{2,1,0:T(8,128)S(1)} collective-permute-done((f32[6,384,128]{2,1,0:T(8,128)S(1)}, f32[6,384,128]{2,1,0:T(8,128)S(1)}, u32[]{:S(2)}, u32[]{:S(2)}) %collective-permute-start.1) | collective-permute-done | bytes 1179680 | tf_op jit(solution)/shard_map/ppermute | solution.py:300
  61.7 3.6 %shard_map.57 = (f32[8,384,128]{2,1,0:T(8,128)S(1)}, f32[6,384,128]{2,1,0:T(8,128)S(1)}, f32[6,384,128]{2,1,0:T(8,128)S(1)}) custom-call(f32[8,408,128]{2,1,0:T(8,128)S(1)} %all_to_all.10.own, f32[6,384,128]{2,1,0:T(8,128)S(1)} %collective-permute-done.lo, f32[6,384,128]{2,1,0:T(8,128)S(1)} %collective-permute-done.1.hi, ...), custom_call_target="tpu_custom_call" | custom-call | tf_op jit(solution)/shard_map/pallas_call | solution.py:249
  65.3 4.7 %collective-permute-start.2 = (f32[6,384,128]{2,1,0:T(8,128)S(1)}, f32[6,384,128]{2,1,0:T(8,128)S(1)}, u32[]{:S(2)}, u32[]{:S(2)}) collective-permute-start(f32[6,384,128]{2,1,0:T(8,128)S(1)} %get-tuple-element.17), channel_id=1, source_target_pairs={{0,96},{1,5},{2,98},{3,7},{4,100},{5,9},{6,102},{7,11},{8,104},{9,... | collective-permute-start | bytes 3538952 | tf_op jit(solution)/shard_map/ppermute | solution.py:306
  70.0 1.9 %collective-permute-start.3 = (f32[6,384,128]{2,1,0:T(8,128)S(1)}, f32[6,384,128]{2,1,0:T(8,128)S(1)}, u32[]{:S(2)}, u32[]{:S(2)}) collective-permute-start(f32[6,384,128]{2,1,0:T(8,128)S(1)} %get-tuple-element.18), channel_id=1, source_target_pairs={{0,672},{1,45},{2,674},{3,47},{4,676},{5,1},{6,678},{7,3},{8,680},... | collective-permute-start | bytes 3538952 | tf_op jit(solution)/shard_map/ppermute | solution.py:307
  71.9 11.8 %collective-permute-done.2.lo = f32[6,384,128]{2,1,0:T(8,128)S(1)} collective-permute-done((f32[6,384,128]{2,1,0:T(8,128)S(1)}, f32[6,384,128]{2,1,0:T(8,128)S(1)}, u32[]{:S(2)}, u32[]{:S(2)}) %collective-permute-start.2) | collective-permute-done | bytes 1179680 | tf_op jit(solution)/shard_map/ppermute | solution.py:306
  83.7 5.6 %collective-permute-done.3.hi = f32[6,384,128]{2,1,0:T(8,128)S(1)} collective-permute-done((f32[6,384,128]{2,1,0:T(8,128)S(1)}, f32[6,384,128]{2,1,0:T(8,128)S(1)}, u32[]{:S(2)}, u32[]{:S(2)}) %collective-permute-start.3) | collective-permute-done | bytes 1179680 | tf_op jit(solution)/shard_map/ppermute | solution.py:307
  89.3 1.9 %shard_map.58 = f32[8,384,128]{2,1,0:T(8,128)S(1)} custom-call(f32[8,384,128]{2,1,0:T(8,128)S(1)} %get-tuple-element.16.own, f32[6,384,128]{2,1,0:T(8,128)S(1)} %collective-permute-done.2.lo, f32[6,384,128]{2,1,0:T(8,128)S(1)} %collective-permute-done.3.hi, f32[64,256]{1,0:T(8,128)S(1)} %get-tuple-element.14.ym, f32[96,256]{1,0:T(8,128)S(1)} %get-tuple-element.15.xm), custom_call_target="tpu_custom_call" | custom-call | tf_op jit(solution)/shard_map/pallas_call | solution.py:249
  91.2 0.0 copy-start.1
  91.2 24.2 %all_to_all.11.got = f32[8,384,128]{2,1,0:T(8,128)S(1)} all-to-all(f32[8,384,128]{2,1,0:T(8,128)S(1)} %shard_map.58), channel_id=1, replica_groups={{0,1,2,3,48,49,50,51},{4,5,6,7,52,53,54,55},{8,9,10,11,56,57,58,59},{12..., dimensions={0} | all-to-all | bytes 3145728 | tf_op jit(solution)/shard_map/all_to_all | solution.py:309
  115.4 0.0 copy-done.1
  115.4 1.6 %shard_map.59 = f32[768,512]{1,0:T(8,128)} custom-call(f32[8,384,128]{2,1,0:T(8,128)S(1)} %all_to_all.11.got, f32[768,512]{1,0:T(8,128)S(1)} %bitcast.3), custom_call_target="tpu_custom_call" | custom-call | tf_op jit(solution)/shard_map/pallas_call | solution.py:249
Async XLA Ops:
  4.2 26.9 %copy-start = (f32[768,768]{1,0:T(8,128)S(1)}, f32[768,768]{1,0:T(8,128)}, u32[]{:S(2)}) copy-start(f32[768,768]{1,0:T(8,128)} %y_ref.1) | copy-start | bytes 7077892
  31.4 28.8 %collective-permute-start = (f32[6,384,128]{2,1,0:T(8,128)S(1)}, f32[6,384,128]{2,1,0:T(8,128)S(1)}, u32[]{:S(2)}, u32[]{:S(2)}) collective-permute-start(f32[6,384,128]{2,1,0:T(8,128)S(1)} %get-tuple-element.12), channel_id=1, source_target_pairs={{0,4},{1,97},{2,6},{3,99},{4,8},{5,101},{6,10},{7,103},{8,12},{9,1... | collective-permute-start | bytes 3538952 | tf_op jit(solution)/shard_map/ppermute | solution.py:299
  35.7 25.9 %collective-permute-start.1 = (f32[6,384,128]{2,1,0:T(8,128)S(1)}, f32[6,384,128]{2,1,0:T(8,128)S(1)}, u32[]{:S(2)}, u32[]{:S(2)}) collective-permute-start(f32[6,384,128]{2,1,0:T(8,128)S(1)} %get-tuple-element.13), channel_id=1, source_target_pairs={{0,44},{1,673},{2,46},{3,675},{4,0},{5,677},{6,2},{7,679},{8,4},{9... | collective-permute-start | bytes 3538952 | tf_op jit(solution)/shard_map/ppermute | solution.py:300
  65.3 18.4 %collective-permute-start.2 = (f32[6,384,128]{2,1,0:T(8,128)S(1)}, f32[6,384,128]{2,1,0:T(8,128)S(1)}, u32[]{:S(2)}, u32[]{:S(2)}) collective-permute-start(f32[6,384,128]{2,1,0:T(8,128)S(1)} %get-tuple-element.17), channel_id=1, source_target_pairs={{0,96},{1,5},{2,98},{3,7},{4,100},{5,9},{6,102},{7,11},{8,104},{9,... | collective-permute-start | bytes 3538952 | tf_op jit(solution)/shard_map/ppermute | solution.py:306
  70.0 19.3 %collective-permute-start.3 = (f32[6,384,128]{2,1,0:T(8,128)S(1)}, f32[6,384,128]{2,1,0:T(8,128)S(1)}, u32[]{:S(2)}, u32[]{:S(2)}) collective-permute-start(f32[6,384,128]{2,1,0:T(8,128)S(1)} %get-tuple-element.18), channel_id=1, source_target_pairs={{0,672},{1,45},{2,674},{3,47},{4,676},{5,1},{6,678},{7,3},{8,680},... | collective-permute-start | bytes 3538952 | tf_op jit(solution)/shard_map/ppermute | solution.py:307
  91.2 24.2 %copy-start.1 = (f32[16,48,512]{2,1,0:T(8,128)S(1)}, f32[16,48,512]{2,1,0:T(8,128)}, u32[]{:S(2)}) copy-start(f32[16,48,512]{2,1,0:T(8,128)} %param.9) | copy-start | bytes 4718596

commit v4 on v3

v4 whole, which is shorter than its diff:
```python
import functools

import jax
import jax.numpy as jnp
from jax import lax
from jax.experimental import pallas as pl
from jax.experimental.pallas import tpu as pltpu
from jax.sharding import PartitionSpec as P

AXES = ("blk", "grp")
ROWS = 384
EXTRA = 24
INTERPRET = False
Y_UNROLL = 2
X_UNROLL = 4
Z_PAIRS = 2
Z_WAIT = 4
VMEM_LIMIT = 24 * 2**20


def split(v):
    hi = v.astype(jnp.bfloat16)
    return hi, (v - hi.astype(jnp.float32)).astype(jnp.bfloat16)


def dot3(a, b, dims):
    (ah, al), (bh, bl) = a, b
    mul = lambda p, q: lax.dot_general(p, q, (dims, ((), ())), preferred_element_type=jnp.float32)
    return mul(ah, bh) + (mul(ah, bl) + mul(al, bh))


def stack(m):
    return jnp.concatenate(split(m), axis=0)


def factor_dot(m, cols):
    n = m.shape[0] // 2
    ch, cl = split(cols)
    mul = lambda p, q: lax.dot_general(p, q, (((1,), (0,)), ((), ())), preferred_element_type=jnp.float32)
    both = mul(m, ch)
    return both[:n] + (both[n:] + mul(m[:n], cl))


def halves(a, b, low):
    return jnp.where(low, a, pltpu.roll(b, 64, 1)), jnp.where(low, pltpu.roll(a, 64, 1), b)


def core_of():
    return lax.rem(lax.axis_index("grp"), 2)


def low_lanes(rows):
    return lax.broadcasted_iota(jnp.int32, (rows, 128), 1) < 64


class Pair:
    def __init__(self, *copies):
        self.copies = copies

    def start(self):
        for c in self.copies:
            c.start()

    def wait(self):
        for c in self.copies:
            c.wait()


def beside(rows, t, low):
    tile = lambda k: rows[:, 128 * (k % 4) : 128 * (k % 4) + 128]
    return jnp.concatenate([tile(t), jnp.where(low, tile(t + 1), tile(t - 1))], axis=1)


def depth_kernel(field_hbm, z_hbm, panel_hbm, out_ref, field_ref, z_ref, w_ref, panel_ref, sems):
    panel_copy = pltpu.make_async_copy(panel_hbm, panel_ref, sems.at[18])
    field_copies, z_copies = [], []
    for u in range(2):
        at = pl.ds(256 * u, 256)
        z_copies.append(pltpu.make_async_copy(z_hbm.at[at, :], z_ref.at[at, :], sems.at[16 + u]))
    for y in range(8):
        for i in range(2):
            at = pl.ds(48 * (8 * i + y), 48)
            field_copies.append(pltpu.make_async_copy(field_hbm.at[at, :], field_ref.at[at, :], sems.at[2 * y + i]))
    field_copies = [Pair(*field_copies[2 * y : 2 * y + 2]) for y in range(8)]
    for c in z_copies + field_copies + [panel_copy]:
        c.start()

    for c in z_copies:
        c.wait()
    for t in range(4):
        both = split(beside(z_ref[pl.ds(128 * t, 128), :], t, low_lanes(128)))
        w_ref[t] = jnp.concatenate(both, axis=0)
    low = low_lanes(48)
    for m in range(8 // Z_PAIRS):
        ys = [Z_PAIRS * m + i for i in range(Z_PAIRS)]
        if (Z_PAIRS * m) % Z_WAIT == 0:
            for c in field_copies[Z_PAIRS * m : Z_PAIRS * m + Z_WAIT]:
                c.wait()
        ys = ys + [8 + y for y in ys]
        n = 48 * len(ys)
        rows = jnp.concatenate([field_ref[pl.ds(48 * y, 48), :] for y in ys], axis=0)
        for t in range(4):
            r = lax.dot_general(
                jnp.concatenate(split(beside(rows, t, low_lanes(n))), axis=0), w_ref[t],
                (((1,), (1,)), ((), ())), preferred_element_type=jnp.float32,
            )
            tile = r[:n, :128] + (r[:n, 128:] + r[n:, :128])
            d = 2 * t
            for i, y in enumerate(ys):
                part = tile[48 * i : 48 * i + 48]
                e = jnp.where(low_lanes(24), part[:24], pltpu.roll(part[24:], 64, 1))
                out_ref[d, pl.ds(y, 24, stride=16), :] = e
            for i in range(Z_PAIRS):
                a = tile[48 * i : 48 * i + 48]
                b = tile[48 * (Z_PAIRS + i) : 48 * (Z_PAIRS + i) + 48]
                out_ref[d + 1, pl.ds(48 * ys[i], 48), :] = jnp.where(low, pltpu.roll(a, 64, 1), b)

    panel_copy.wait()
    share = lax.rem(lax.axis_index("grp"), 4)
    for s in range(4):
        @pl.when(share == s)
        def _():
            rows = panel_ref[pl.ds(12 * s, 12), :]
            for d in range(8):
                out_ref[d, pl.ds(ROWS, 12), :] = rows[:, :128]
                out_ref[d, pl.ds(ROWS + 12, 12), pl.ds(0, 16)] = rows[:, 128:]


def loop(count, unroll, body):
    def step(i, carry):
        for k in range(unroll):
            body(unroll * i + k)
        return carry

    lax.fori_loop(0, count // unroll, step, 0)


def pair_of(body):
    return [body(0), body(1)]


def y_rows(x):
    return pl.ds(pl.multiple_of(16 * x, 16), 16)


def x_rows(y):
    return pl.ds(pl.multiple_of(48 * y, 16), 48)


def keep(part, at, n, r):
    for j in range(2):
        part[pl.ds(pl.multiple_of(n * (at + j), 32), n), :] = r[:, 128 * j : 128 * j + 128]


def part_rows(part, at, n):
    return part[pl.ds(pl.multiple_of(n * at, 32), n), :]


def lower_kernel(y_core, own, lo, ym, xm, part):
    core = core_of()

    @pl.when(core == y_core)
    def _():
        ys = stack(ym[:, :112])
        for xh in range(2):
            def body(i):
                def column(j):
                    at = y_rows(2 * i + j)
                    return jnp.concatenate(
                        [lo[3 * xh + s, at, :] for s in range(3)] + [own[4 * xh + s, at, :] for s in range(4)], axis=0
                    )

                keep(part, 24 * xh + 2 * i, 64, factor_dot(ys, jnp.concatenate(pair_of(column), axis=1)))

            loop(12, Y_UNROLL, body)

    @pl.when(core != y_core)
    def _():
        xs = stack(xm[:, :144])
        for s in range(4):
            def body(i):
                def column(j):
                    at = x_rows(2 * i + j)
                    return jnp.concatenate([lo[s, at, :], own[s, at, :], own[4 + s, at, :]], axis=0)

                keep(part, 8 * s + 2 * i, 96, factor_dot(xs, jnp.concatenate(pair_of(column), axis=1)))

            loop(4, X_UNROLL, body)


def y_finish(part, hi, ym, emit):
    ys = stack(ym[:, 128:176])
    for xh in range(2):
        def body(i):
            def column(j):
                return jnp.concatenate([hi[3 * xh + s, y_rows(2 * i + j), :] for s in range(3)], axis=0)

            r = factor_dot(ys, jnp.concatenate(pair_of(column), axis=1))
            for j in range(2):
                x = 2 * i + j
                emit(xh, x, part_rows(part, 24 * xh + x, 64) + r[:, 128 * j : 128 * j + 128])

        loop(12, Y_UNROLL, body)


def x_finish(part, hi, xu, emit):
    xs = stack(xu[:, :48])
    for s in range(4):
        def body(i):
            r = factor_dot(xs, jnp.concatenate(pair_of(lambda j: hi[s, x_rows(2 * i + j), :]), axis=1))
            for j in range(2):
                y = 2 * i + j
                p = part_rows(part, 8 * s + y, 96)
                emit(s, y, (p[:48], p[48:] + r[:, 128 * j : 128 * j + 128]))

        loop(4, X_UNROLL, body)


def pick_kernel(own, y_ref, plus, minus, ym, xm, xu):
    core = core_of()
    slab = lax.div(lax.axis_index("grp"), 4)
    ny = y_ref.shape[0]
    @pl.when(core == 0)
    def _():
        for i, (p, m) in enumerate(((1, 0), (2, 1), (3, 2), (5, 4), (6, 5), (7, 6))):
            plus[i] = own[p, pl.ds(0, ROWS), :]
            minus[i] = own[m, pl.ds(0, ROWS), :]

    @pl.when(core == 1)
    def _():
        for s in range(4):
            plus[s] = own[4 + s, pl.ds(0, ROWS), :]
            minus[s] = own[s, pl.ds(0, ROWS), :]

    few = lax.broadcasted_iota(jnp.int32, (12, 128), 1) < 16
    for xh in range(2):
        for s in range(4):
            p = own[4 * xh + s, pl.ds(ROWS, 12), :]
            q = jnp.where(few, own[4 * xh + s, pl.ds(ROWS + 12, 12), :], 0.0)
            w = jnp.concatenate([p, q], axis=1)
            xm[pl.ds(48 * xh + 12 * s, 12), :] = pltpu.roll(w, 48, 1) if xh else w
            if xh:
                xu[pl.ds(12 * s, 12), :] = pltpu.roll(w, 160, 1)[:, :128]
    rows = y_ref[pl.ds(pl.multiple_of(64 * slab, 64), 64), :]
    for i, first in enumerate((-48, 64)):
        shift = lax.rem(2 * ny - first - 64 * slab, ny)
        ym[:, pl.ds(128 * i, 128)] = pltpu.roll(rows, shift, 1)[:, :128]


def first_kernel(part, hi, ym, xu, out, plus, minus):
    core = core_of()

    @pl.when(core == 0)
    def _():
        def emit(xh, xx, r):
            for s in range(4):
                w = halves(r[16 * s : 16 * s + 8], r[16 * s + 8 : 16 * s + 16], low_lanes(8))
                for h in range(2):
                    out[4 * xh + s, pl.ds(24 * h + xx, 8, stride=48), :] = w[h]

        y_finish(part, hi, ym, emit)
        for s in range(4):
            plus[s] = out[4 + s]
            minus[s] = out[s]

    @pl.when(core == 1)
    def _():
        def emit(s, yy, r):
            for xh in range(2):
                q = halves(r[xh][:24], r[xh][24:], low_lanes(24))
                for yh in range(2):
                    out[4 * xh + s, pl.ds(8 * yh + yy, 24, stride=16), :] = q[yh]

        x_finish(part, hi, xu, emit)
        for xh in range(2):
            for s in range(3):
                plus[3 * xh + s] = out[4 * xh + s + 1]
                minus[3 * xh + s] = out[4 * xh + s]


def second_kernel(part, hi, ym, xu, out):
    core = core_of()

    @pl.when(core == 0)
    def _():
        def emit(s, yy, r):
            for xh in range(2):
                out[4 * xh + s, x_rows(yy), :] = r[xh]

        x_finish(part, hi, xu, emit)

    @pl.when(core == 1)
    def _():
        def emit(xh, xx, r):
            for s in range(4):
                out[4 * xh + s, y_rows(xx), :] = r[16 * s : 16 * s + 16]

        y_finish(part, hi, ym, emit)


def last_kernel(got, scale_ref, out_ref):
    low = low_lanes(24)
    for t in range(4):
        lanes = pl.ds(128 * t, 128)
        for yy in range(8):
            a = got[2 * t, pl.ds(48 * yy, 48), :]
            for yh in range(2):
                y = 8 * yh + yy
                c = got[2 * t + 1, pl.ds(y, 24, stride=16), :]
                c2 = pltpu.roll(c, 64, 1)
                a2 = pltpu.roll(a, 64, 1) if yh else a
                for h in range(2):
                    at = pl.ds(48 * y + 24 * h, 24)
                    r = jnp.where(low, a2[24 * h : 24 * h + 24], c if h else c2)
                    out_ref[at, lanes] = r * scale_ref[at, lanes]


def call(kernel, shapes, *args, hbm=(), plain=False, scratch=()):
    vmem = pl.BlockSpec(memory_space=pltpu.VMEM)
    outs = [jax.ShapeDtypeStruct(s, jnp.float32) for s in shapes]
    if not INTERPRET:
        args = [pltpu.with_memory_space_constraint(a, pltpu.HBM if i in hbm else pltpu.VMEM) for i, a in enumerate(args)]
        if not plain:
            outs = [pltpu.VMEM(s, jnp.float32) for s in shapes]
    return pl.pallas_call(
        kernel,
        out_shape=outs,
        in_specs=[pl.BlockSpec(memory_space=pltpu.HBM) if i in hbm else vmem for i in range(len(args))],
        out_specs=[vmem for _ in shapes],
        scratch_shapes=list(scratch),
        compiler_params=pltpu.CompilerParams(vmem_limit_bytes=VMEM_LIMIT),
        interpret=INTERPRET,
    )(*args)


def links(mesh):
    n_blk, n_grp = mesh.shape["blk"], mesh.shape["grp"]
    n_y, n_z = n_blk // 2, n_grp // 4

    def place(y, xh, z, r):
        return ((y % n_y) * 2 + xh) * n_grp + (z % n_z) * 4 + r

    everyone = [(y, xh, z, r) for y in range(n_y) for xh in range(2) for z in range(n_z) for r in range(4)]

    def hop(step, along_z):
        pairs = []
        for y, xh, z, r in everyone:
            if r % 2 == along_z:
                to = place(y, xh, z + step, r)
            else:
                to = place(y + step, xh, z, r)
            pairs.append((place(y, xh, z, r), to))
        return pairs

    eights = [[place(y, xh, z, r) for xh in range(2) for r in range(4)] for y in range(n_y) for z in range(n_z)]
    return eights, hop


def on_device(eights, hop, field, x_panel, y_factor, z_factor, scaling):
    (sent,) = call(
        depth_kernel, [(8, ROWS + EXTRA, 128)], field.reshape(768, 512), z_factor, x_panel,
        hbm=(0, 1, 2),
        scratch=[
            pltpu.VMEM((768, 512), jnp.float32),
            pltpu.VMEM((512, 512), jnp.float32),
            pltpu.VMEM((4, 256, 256), jnp.bfloat16),
            pltpu.VMEM((48, 144), jnp.float32),
            pltpu.SemaphoreType.DMA((19,)),
        ],
    )
    got = lax.all_to_all(sent, AXES, split_axis=0, concat_axis=0, tiled=True, axis_index_groups=eights)

    plus, minus, ym, xm, xu = call(
        pick_kernel, [(6, ROWS, 128), (6, ROWS, 128), (64, 256), (96, 256), (48, 128)], got, y_factor
    )
    lo = lax.ppermute(plus, AXES, hop(1, 0))
    hi = lax.ppermute(minus, AXES, hop(-1, 0))
    (part,) = call(functools.partial(lower_kernel, 0), [(8 * ROWS, 128)], got, lo, ym, xm)
    own, plus, minus = call(
        first_kernel, [(8, ROWS, 128), (6, ROWS, 128), (6, ROWS, 128)], part, hi, ym, xu
    )
    lo = lax.ppermute(plus, AXES, hop(1, 1))
    hi = lax.ppermute(minus, AXES, hop(-1, 1))
    (part,) = call(functools.partial(lower_kernel, 1), [(8 * ROWS, 128)], own, lo, ym, xm)
    (sent,) = call(second_kernel, [(8, ROWS, 128)], part, hi, ym, xu)
    got = lax.all_to_all(sent, AXES, split_axis=0, concat_axis=0, tiled=True, axis_index_groups=eights)
    (out,) = call(last_kernel, [(768, 512)], got, scaling.reshape(768, 512), plain=True)
    return out.reshape(16, 48, 512)


def solution(mesh):
    eights, hop = links(mesh)
    in_specs = (P("grp", "blk", None), P("blk", None), P(), P(), P("grp", "blk", None))
    return jax.shard_map(
        functools.partial(on_device, eights, hop),
        mesh=mesh,
        in_specs=in_specs,
        out_specs=P("grp", "blk", None),
        check_vma=False,
    )
```

time: 117 us -> 116 us (level)
  waiting for transfers between devices: 31.1 us -> 28.8 us
    ppermute x1, waiting for transfers between devices: 1.46 us -> 0.01 us  [on_device(): hi = lax.ppermute(minus, AXES, hop(-1, 0))]
    pallas_call x5 -> x7, Pallas kernels: 11.7 us -> 12.2 us  [call(): pl.pallas_call(kernel, out_shape=outs, in_specs=[pl.BlockSpec(memory_spac...]
  transfers between devices with their start and end apart: 4 -> 4, of which waited for: 4 -> 3; matrix products, arithmetic and copies ran while one was open for 0% -> 0% of each run, Pallas kernels for 0% -> 3%
where the time goes in v4:
time: 116 us; the launch traced here: 115 us
  blocking collectives  51 us (44%)
  waiting for transfers between devices  28.8 us (25%)
  starting transfers between devices  23.1 us (20%)
  Pallas kernels  12.2 us (11%)
    all_to_all x2, blocking collectives, on_device(): lax.all_to_all(sent, AXES, split_axis=0, concat_axis=0, tiled=True, axis_...  51 us
    ppermute x1, waiting for transfers between devices, on_device(): lo = lax.ppermute(plus, AXES, hop(1, 0))  12.2 us
    pallas_call x7, Pallas kernels, call(): pl.pallas_call(kernel, out_shape=outs, in_specs=[pl.BlockSpec(memory_spac...  12.2 us
    ppermute x1, starting transfers between devices, on_device(): hi = lax.ppermute(minus, AXES, hop(-1, 0))  12.2 us
    ppermute x1, waiting for transfers between devices, on_device(): lo = lax.ppermute(plus, AXES, hop(1, 1))  11.8 us
    ppermute x1, waiting for transfers between devices, on_device(): hi = lax.ppermute(minus, AXES, hop(-1, 1))  4.83 us
    ppermute x1, starting transfers between devices, on_device(): lo = lax.ppermute(plus, AXES, hop(1, 1))  4.64 us
    ppermute x1, starting transfers between devices, on_device(): lo = lax.ppermute(plus, AXES, hop(1, 0))  4.28 us
  transfers between devices with their start and end apart: 4, of which 3 were waited for; matrix products, arithmetic and copies ran while one was open for 0% of the time, Pallas kernels for 3%

profile of v4, /device:TPU:24, one launch (start us, length us, event | category | flops | bytes accessed | tf_op | source)
XLA Modules:
  0.0 115.3 jit_solution(12268801699267744825)
XLA Ops:
  0.0 3.2 %shard_map.55 = f32[8,408,128]{2,1,0:T(8,128)S(1)} custom-call(f32[768,512]{1,0:T(8,128)} %bitcast.4, f32[512,512]{1,0:T(8,128)} %z_hbm.1, f32[48,144]{1,0:T(8,128)} %panel_hbm.1), custom_call_target="tpu_custom_call" | custom-call | tf_op jit(solution)/shard_map/pallas_call | solution.py:325
  3.2 0.0 copy-start
  3.2 26.9 %all_to_all.10.own = f32[8,408,128]{2,1,0:T(8,128)S(1)} all-to-all(f32[8,408,128]{2,1,0:T(8,128)S(1)} %shard_map.55), channel_id=1, replica_groups={{0,1,2,3,48,49,50,51},{4,5,6,7,52,53,54,55},{8,9,10,11,56,57,58,59},{12..., dimensions={0} | all-to-all | bytes 3342336 | tf_op jit(solution)/shard_map/all_to_all | solution.py:371
  30.1 0.0 copy-done
  30.1 0.4 shard_map.56
  30.5 4.3 %collective-permute-start = (f32[6,384,128]{2,1,0:T(8,128)S(1)}, f32[6,384,128]{2,1,0:T(8,128)S(1)}, u32[]{:S(2)}, u32[]{:S(2)}) collective-permute-start(f32[6,384,128]{2,1,0:T(8,128)S(1)} %get-tuple-element.13), channel_id=1, source_target_pairs={{0,4},{1,97},{2,6},{3,99},{4,8},{5,101},{6,10},{7,103},{8,12},{9,1... | collective-permute-start | bytes 3538952 | tf_op jit(solution)/shard_map/ppermute | solution.py:376
  34.8 12.2 %collective-permute-start.1 = (f32[6,384,128]{2,1,0:T(8,128)S(1)}, f32[6,384,128]{2,1,0:T(8,128)S(1)}, u32[]{:S(2)}, u32[]{:S(2)}) collective-permute-start(f32[6,384,128]{2,1,0:T(8,128)S(1)} %get-tuple-element.16), channel_id=1, source_target_pairs={{0,44},{1,673},{2,46},{3,675},{4,0},{5,677},{6,2},{7,679},{8,4},{9... | collective-permute-start | bytes 3538952 | tf_op jit(solution)/shard_map/ppermute | solution.py:377
  47.0 12.2 %collective-permute-done.lo = f32[6,384,128]{2,1,0:T(8,128)S(1)} collective-permute-done((f32[6,384,128]{2,1,0:T(8,128)S(1)}, f32[6,384,128]{2,1,0:T(8,128)S(1)}, u32[]{:S(2)}, u32[]{:S(2)}) %collective-permute-start) | collective-permute-done | bytes 1179680 | tf_op jit(solution)/shard_map/ppermute | solution.py:376
  59.2 2.4 %shard_map.57.part = f32[3072,128]{1,0:T(8,128)S(1)} custom-call(f32[8,408,128]{2,1,0:T(8,128)S(1)} %all_to_all.10.own, f32[6,384,128]{2,1,0:T(8,128)S(1)} %collective-permute-done.lo, f32[64,256]{1,0:T(8,128)S(1)} %get-tuple-element.14.ym, f32[96,256]{1,0:T(8,128)S(1)} %get-tuple-element.15.xm), custom_call_target="tpu_custom_call" | custom-call | tf_op jit(solution)/shard_map/pallas_call | solution.py:325
  61.6 0.0 collective-permute-done.1.hi
  61.6 3.4 %shard_map.58 = (f32[8,384,128]{2,1,0:T(8,128)S(1)}, f32[6,384,128]{2,1,0:T(8,128)S(1)}, f32[6,384,128]{2,1,0:T(8,128)S(1)}) custom-call(f32[3072,128]{1,0:T(8,128)S(1)} %shard_map.57.part, f32[6,384,128]{2,1,0:T(8,128)S(1)} %collective-permute-done.1.hi, f32[64,256]{1,0:T(8,128)S(1)} %get-tuple-element.14.ym, f32[48,128]{1,0:T(8,128)S(1)} %get-tuple-element.17.xu), custom_call_target="tpu_custom_call" | custom-call | tf_op jit(solution)/shard_map/pallas_call | solution.py:325
  65.1 4.6 %collective-permute-start.2 = (f32[6,384,128]{2,1,0:T(8,128)S(1)}, f32[6,384,128]{2,1,0:T(8,128)S(1)}, u32[]{:S(2)}, u32[]{:S(2)}) collective-permute-start(f32[6,384,128]{2,1,0:T(8,128)S(1)} %get-tuple-element.19), channel_id=1, source_target_pairs={{0,96},{1,5},{2,98},{3,7},{4,100},{5,9},{6,102},{7,11},{8,104},{9,... | collective-permute-start | bytes 3538952 | tf_op jit(solution)/shard_map/ppermute | solution.py:382
  69.7 1.9 %collective-permute-start.3 = (f32[6,384,128]{2,1,0:T(8,128)S(1)}, f32[6,384,128]{2,1,0:T(8,128)S(1)}, u32[]{:S(2)}, u32[]{:S(2)}) collective-permute-start(f32[6,384,128]{2,1,0:T(8,128)S(1)} %get-tuple-element.20), channel_id=1, source_target_pairs={{0,672},{1,45},{2,674},{3,47},{4,676},{5,1},{6,678},{7,3},{8,680},... | collective-permute-start | bytes 3538952 | tf_op jit(solution)/shard_map/ppermute | solution.py:383
  71.6 11.8 %collective-permute-done.2.lo = f32[6,384,128]{2,1,0:T(8,128)S(1)} collective-permute-done((f32[6,384,128]{2,1,0:T(8,128)S(1)}, f32[6,384,128]{2,1,0:T(8,128)S(1)}, u32[]{:S(2)}, u32[]{:S(2)}) %collective-permute-start.2) | collective-permute-done | bytes 1179680 | tf_op jit(solution)/shard_map/ppermute | solution.py:382
  83.4 0.8 shard_map.59.part
  84.2 4.8 %collective-permute-done.3.hi = f32[6,384,128]{2,1,0:T(8,128)S(1)} collective-permute-done((f32[6,384,128]{2,1,0:T(8,128)S(1)}, f32[6,384,128]{2,1,0:T(8,128)S(1)}, u32[]{:S(2)}, u32[]{:S(2)}) %collective-permute-start.3) | collective-permute-done | bytes 1179680 | tf_op jit(solution)/shard_map/ppermute | solution.py:383
  89.0 0.5 shard_map.60
  89.5 0.0 copy-start.1
  89.5 24.2 %all_to_all.11.got = f32[8,384,128]{2,1,0:T(8,128)S(1)} all-to-all(f32[8,384,128]{2,1,0:T(8,128)S(1)} %shard_map.60), channel_id=1, replica_groups={{0,1,2,3,48,49,50,51},{4,5,6,7,52,53,54,55},{8,9,10,11,56,57,58,59},{12..., dimensions={0} | all-to-all | bytes 3145728 | tf_op jit(solution)/shard_map/all_to_all | solution.py:386
  113.7 0.0 copy-done.1
  113.7 1.6 %shard_map.61 = f32[768,512]{1,0:T(8,128)} custom-call(f32[8,384,128]{2,1,0:T(8,128)S(1)} %all_to_all.11.got, f32[768,512]{1,0:T(8,128)S(1)} %bitcast.3), custom_call_target="tpu_custom_call" | custom-call | tf_op jit(solution)/shard_map/pallas_call | solution.py:325
Async XLA Ops:
  3.2 26.9 %copy-start = (f32[768,768]{1,0:T(8,128)S(1)}, f32[768,768]{1,0:T(8,128)}, u32[]{:S(2)}) copy-start(f32[768,768]{1,0:T(8,128)} %y_ref.1) | copy-start | bytes 7077892
  30.5 28.8 %collective-permute-start = (f32[6,384,128]{2,1,0:T(8,128)S(1)}, f32[6,384,128]{2,1,0:T(8,128)S(1)}, u32[]{:S(2)}, u32[]{:S(2)}) collective-permute-start(f32[6,384,128]{2,1,0:T(8,128)S(1)} %get-tuple-element.13), channel_id=1, source_target_pairs={{0,4},{1,97},{2,6},{3,99},{4,8},{5,101},{6,10},{7,103},{8,12},{9,1... | collective-permute-start | bytes 3538952 | tf_op jit(solution)/shard_map/ppermute | solution.py:376
  34.8 26.9 %collective-permute-start.1 = (f32[6,384,128]{2,1,0:T(8,128)S(1)}, f32[6,384,128]{2,1,0:T(8,128)S(1)}, u32[]{:S(2)}, u32[]{:S(2)}) collective-permute-start(f32[6,384,128]{2,1,0:T(8,128)S(1)} %get-tuple-element.16), channel_id=1, source_target_pairs={{0,44},{1,673},{2,46},{3,675},{4,0},{5,677},{6,2},{7,679},{8,4},{9... | collective-permute-start | bytes 3538952 | tf_op jit(solution)/shard_map/ppermute | solution.py:377
  65.1 18.3 %collective-permute-start.2 = (f32[6,384,128]{2,1,0:T(8,128)S(1)}, f32[6,384,128]{2,1,0:T(8,128)S(1)}, u32[]{:S(2)}, u32[]{:S(2)}) collective-permute-start(f32[6,384,128]{2,1,0:T(8,128)S(1)} %get-tuple-element.19), channel_id=1, source_target_pairs={{0,96},{1,5},{2,98},{3,7},{4,100},{5,9},{6,102},{7,11},{8,104},{9,... | collective-permute-start | bytes 3538952 | tf_op jit(solution)/shard_map/ppermute | solution.py:382
  69.7 19.3 %collective-permute-start.3 = (f32[6,384,128]{2,1,0:T(8,128)S(1)}, f32[6,384,128]{2,1,0:T(8,128)S(1)}, u32[]{:S(2)}, u32[]{:S(2)}) collective-permute-start(f32[6,384,128]{2,1,0:T(8,128)S(1)} %get-tuple-element.20), channel_id=1, source_target_pairs={{0,672},{1,45},{2,674},{3,47},{4,676},{5,1},{6,678},{7,3},{8,680},... | collective-permute-start | bytes 3538952 | tf_op jit(solution)/shard_map/ppermute | solution.py:383
  89.5 24.2 %copy-start.1 = (f32[16,48,512]{2,1,0:T(8,128)S(1)}, f32[16,48,512]{2,1,0:T(8,128)}, u32[]{:S(2)}) copy-start(f32[16,48,512]{2,1,0:T(8,128)} %param.9) | copy-start | bytes 4718596

commit v5 on v4

--- a/solution.py
+++ b/solution.py
@@ -11,7 +11,7 @@
 ROWS = 384
 EXTRA = 24
 INTERPRET = False
-Y_UNROLL = 2
+Y_UNROLL = 12
 X_UNROLL = 4
 Z_PAIRS = 2
 Z_WAIT = 4

time: 116 us -> 112 us (0.966)
  Pallas kernels: 12.2 us -> 8.22 us
    pallas_call x7, Pallas kernels: 12.2 us -> 8.22 us  [call(): pl.pallas_call(kernel, out_shape=outs, in_specs=[pl.BlockSpec(memory_spac...]
  transfers between devices with their start and end apart: 4 -> 4, of which waited for: 3 -> 4; matrix products, arithmetic and copies ran while one was open for 0% -> 0% of each run, Pallas kernels for 3% -> 1%
where the time goes in v5:
time: 112 us
  blocking collectives  51 us (46%)
  waiting for transfers between devices  29.5 us (26%)
  starting transfers between devices  23.1 us (21%)
  Pallas kernels  8.22 us (7%)
    all_to_all x2, blocking collectives, on_device(): lax.all_to_all(sent, AXES, split_axis=0, concat_axis=0, tiled=True, axis_...  51 us
    ppermute x1, waiting for transfers between devices, on_device(): lo = lax.ppermute(plus, AXES, hop(1, 0))  12.2 us
    ppermute x1, starting transfers between devices, on_device(): hi = lax.ppermute(minus, AXES, hop(-1, 0))  12.2 us
    ppermute x1, waiting for transfers between devices, on_device(): lo = lax.ppermute(plus, AXES, hop(1, 1))  11.8 us
    pallas_call x7, Pallas kernels, call(): pl.pallas_call(kernel, out_shape=outs, in_specs=[pl.BlockSpec(memory_spac...  8.22 us
    ppermute x1, waiting for transfers between devices, on_device(): hi = lax.ppermute(minus, AXES, hop(-1, 1))  4.84 us
    ppermute x1, starting transfers between devices, on_device(): lo = lax.ppermute(plus, AXES, hop(1, 1))  4.68 us
    ppermute x1, starting transfers between devices, on_device(): lo = lax.ppermute(plus, AXES, hop(1, 0))  4.28 us
  transfers between devices with their start and end apart: 4, of which 4 were waited for; matrix products, arithmetic and copies ran while one was open for 0% of the time, Pallas kernels for 1%

profile of v5, /device:TPU:24, one launch (start us, length us, event | category | flops | bytes accessed | tf_op | source)
XLA Modules:
  0.0 112.0 jit_solution(11912131166434565911)
XLA Ops:
  0.0 3.2 %shard_map.55 = f32[8,408,128]{2,1,0:T(8,128)S(1)} custom-call(f32[768,512]{1,0:T(8,128)} %bitcast.4, f32[512,512]{1,0:T(8,128)} %z_hbm.1, f32[48,144]{1,0:T(8,128)} %panel_hbm.1), custom_call_target="tpu_custom_call" | custom-call | tf_op jit(solution)/shard_map/pallas_call | solution.py:325
  3.2 0.0 copy-start
  3.2 26.9 %all_to_all.10.own = f32[8,408,128]{2,1,0:T(8,128)S(1)} all-to-all(f32[8,408,128]{2,1,0:T(8,128)S(1)} %shard_map.55), channel_id=1, replica_groups={{0,1,2,3,48,49,50,51},{4,5,6,7,52,53,54,55},{8,9,10,11,56,57,58,59},{12..., dimensions={0} | all-to-all | bytes 3342336 | tf_op jit(solution)/shard_map/all_to_all | solution.py:371
  30.1 0.0 copy-done
  30.1 0.4 shard_map.56
  30.5 4.3 %collective-permute-start = (f32[6,384,128]{2,1,0:T(8,128)S(1)}, f32[6,384,128]{2,1,0:T(8,128)S(1)}, u32[]{:S(2)}, u32[]{:S(2)}) collective-permute-start(f32[6,384,128]{2,1,0:T(8,128)S(1)} %get-tuple-element.13), channel_id=1, source_target_pairs={{0,4},{1,97},{2,6},{3,99},{4,8},{5,101},{6,10},{7,103},{8,12},{9,1... | collective-permute-start | bytes 3538952 | tf_op jit(solution)/shard_map/ppermute | solution.py:376
  34.8 12.2 %collective-permute-start.1 = (f32[6,384,128]{2,1,0:T(8,128)S(1)}, f32[6,384,128]{2,1,0:T(8,128)S(1)}, u32[]{:S(2)}, u32[]{:S(2)}) collective-permute-start(f32[6,384,128]{2,1,0:T(8,128)S(1)} %get-tuple-element.16), channel_id=1, source_target_pairs={{0,44},{1,673},{2,46},{3,675},{4,0},{5,677},{6,2},{7,679},{8,4},{9... | collective-permute-start | bytes 3538952 | tf_op jit(solution)/shard_map/ppermute | solution.py:377
  47.0 12.2 %collective-permute-done.lo = f32[6,384,128]{2,1,0:T(8,128)S(1)} collective-permute-done((f32[6,384,128]{2,1,0:T(8,128)S(1)}, f32[6,384,128]{2,1,0:T(8,128)S(1)}, u32[]{:S(2)}, u32[]{:S(2)}) %collective-permute-start) | collective-permute-done | bytes 1179680 | tf_op jit(solution)/shard_map/ppermute | solution.py:376
  59.2 0.8 shard_map.57.part
  60.0 0.7 collective-permute-done.1.hi
  60.7 1.0 shard_map.58
  61.7 4.7 %collective-permute-start.2 = (f32[6,384,128]{2,1,0:T(8,128)S(1)}, f32[6,384,128]{2,1,0:T(8,128)S(1)}, u32[]{:S(2)}, u32[]{:S(2)}) collective-permute-start(f32[6,384,128]{2,1,0:T(8,128)S(1)} %get-tuple-element.19), channel_id=1, source_target_pairs={{0,96},{1,5},{2,98},{3,7},{4,100},{5,9},{6,102},{7,11},{8,104},{9,... | collective-permute-start | bytes 3538952 | tf_op jit(solution)/shard_map/ppermute | solution.py:382
  66.4 1.9 %collective-permute-start.3 = (f32[6,384,128]{2,1,0:T(8,128)S(1)}, f32[6,384,128]{2,1,0:T(8,128)S(1)}, u32[]{:S(2)}, u32[]{:S(2)}) collective-permute-start(f32[6,384,128]{2,1,0:T(8,128)S(1)} %get-tuple-element.20), channel_id=1, source_target_pairs={{0,672},{1,45},{2,674},{3,47},{4,676},{5,1},{6,678},{7,3},{8,680},... | collective-permute-start | bytes 3538952 | tf_op jit(solution)/shard_map/ppermute | solution.py:383
  68.3 11.8 %collective-permute-done.2.lo = f32[6,384,128]{2,1,0:T(8,128)S(1)} collective-permute-done((f32[6,384,128]{2,1,0:T(8,128)S(1)}, f32[6,384,128]{2,1,0:T(8,128)S(1)}, u32[]{:S(2)}, u32[]{:S(2)}) %collective-permute-start.2) | collective-permute-done | bytes 1179680 | tf_op jit(solution)/shard_map/ppermute | solution.py:382
  80.1 0.8 shard_map.59.part
  80.9 4.8 %collective-permute-done.3.hi = f32[6,384,128]{2,1,0:T(8,128)S(1)} collective-permute-done((f32[6,384,128]{2,1,0:T(8,128)S(1)}, f32[6,384,128]{2,1,0:T(8,128)S(1)}, u32[]{:S(2)}, u32[]{:S(2)}) %collective-permute-start.3) | collective-permute-done | bytes 1179680 | tf_op jit(solution)/shard_map/ppermute | solution.py:383
  85.7 0.5 shard_map.60
  86.2 0.0 copy-start.1
  86.2 24.2 %all_to_all.11.got = f32[8,384,128]{2,1,0:T(8,128)S(1)} all-to-all(f32[8,384,128]{2,1,0:T(8,128)S(1)} %shard_map.60), channel_id=1, replica_groups={{0,1,2,3,48,49,50,51},{4,5,6,7,52,53,54,55},{8,9,10,11,56,57,58,59},{12..., dimensions={0} | all-to-all | bytes 3145728 | tf_op jit(solution)/shard_map/all_to_all | solution.py:386
  110.4 0.0 copy-done.1
  110.4 1.6 %shard_map.61 = f32[768,512]{1,0:T(8,128)} custom-call(f32[8,384,128]{2,1,0:T(8,128)S(1)} %all_to_all.11.got, f32[768,512]{1,0:T(8,128)S(1)} %bitcast.3), custom_call_target="tpu_custom_call" | custom-call | tf_op jit(solution)/shard_map/pallas_call | solution.py:325
Async XLA Ops:
  3.2 26.9 %copy-start = (f32[768,768]{1,0:T(8,128)S(1)}, f32[768,768]{1,0:T(8,128)}, u32[]{:S(2)}) copy-start(f32[768,768]{1,0:T(8,128)} %y_ref.1) | copy-start | bytes 7077892
  30.5 28.8 %collective-permute-start = (f32[6,384,128]{2,1,0:T(8,128)S(1)}, f32[6,384,128]{2,1,0:T(8,128)S(1)}, u32[]{:S(2)}, u32[]{:S(2)}) collective-permute-start(f32[6,384,128]{2,1,0:T(8,128)S(1)} %get-tuple-element.13), channel_id=1, source_target_pairs={{0,4},{1,97},{2,6},{3,99},{4,8},{5,101},{6,10},{7,103},{8,12},{9,1... | collective-permute-start | bytes 3538952 | tf_op jit(solution)/shard_map/ppermute | solution.py:376
  34.8 25.9 %collective-permute-start.1 = (f32[6,384,128]{2,1,0:T(8,128)S(1)}, f32[6,384,128]{2,1,0:T(8,128)S(1)}, u32[]{:S(2)}, u32[]{:S(2)}) collective-permute-start(f32[6,384,128]{2,1,0:T(8,128)S(1)} %get-tuple-element.16), channel_id=1, source_target_pairs={{0,44},{1,673},{2,46},{3,675},{4,0},{5,677},{6,2},{7,679},{8,4},{9... | collective-permute-start | bytes 3538952 | tf_op jit(solution)/shard_map/ppermute | solution.py:377
  61.7 18.4 %collective-permute-start.2 = (f32[6,384,128]{2,1,0:T(8,128)S(1)}, f32[6,384,128]{2,1,0:T(8,128)S(1)}, u32[]{:S(2)}, u32[]{:S(2)}) collective-permute-start(f32[6,384,128]{2,1,0:T(8,128)S(1)} %get-tuple-element.19), channel_id=1, source_target_pairs={{0,96},{1,5},{2,98},{3,7},{4,100},{5,9},{6,102},{7,11},{8,104},{9,... | collective-permute-start | bytes 3538952 | tf_op jit(solution)/shard_map/ppermute | solution.py:382
  66.4 19.3 %collective-permute-start.3 = (f32[6,384,128]{2,1,0:T(8,128)S(1)}, f32[6,384,128]{2,1,0:T(8,128)S(1)}, u32[]{:S(2)}, u32[]{:S(2)}) collective-permute-start(f32[6,384,128]{2,1,0:T(8,128)S(1)} %get-tuple-element.20), channel_id=1, source_target_pairs={{0,672},{1,45},{2,674},{3,47},{4,676},{5,1},{6,678},{7,3},{8,680},... | collective-permute-start | bytes 3538952 | tf_op jit(solution)/shard_map/ppermute | solution.py:383
  86.2 24.2 %copy-start.1 = (f32[16,48,512]{2,1,0:T(8,128)S(1)}, f32[16,48,512]{2,1,0:T(8,128)}, u32[]{:S(2)}) copy-start(f32[16,48,512]{2,1,0:T(8,128)} %param.9) | copy-start | bytes 4718596

commit v6 on v5

--- a/solution.py
+++ b/solution.py
@@ -47,6 +47,20 @@
 
 def core_of():
     return lax.rem(lax.axis_index("grp"), 2)
+
+
+def parities():
+    along_y = lax.rem(lax.div(lax.axis_index("blk"), 2), 2)
+    return along_y, lax.rem(lax.div(lax.axis_index("grp"), 4), 2)
+
+
+def put(first, second, parity, up, down):
+    for p, (u, d) in enumerate(((first, second), (second, first))):
+        @pl.when(parity == p)
+        def _():
+            for i in range(len(up)):
+                u[i] = up[i]()
+                d[i] = down[i]()
 
 
 def low_lanes(rows):
@@ -156,7 +170,7 @@
     return part[pl.ds(pl.multiple_of(n * at, 32), n), :]
 
 
-def lower_kernel(y_core, own, lo, ym, xm, part):
+def lower_kernel(y_core, own, near, ym, xm, part):
     core = core_of()
 
     @pl.when(core == y_core)
@@ -167,7 +181,7 @@
                 def column(j):
                     at = y_rows(2 * i + j)
                     return jnp.concatenate(
-                        [lo[3 * xh + s, at, :] for s in range(3)] + [own[4 * xh + s, at, :] for s in range(4)], axis=0
+                        [near[3 * xh + s, at, :] for s in range(3)] + [own[4 * xh + s, at, :] for s in range(4)], axis=0
                     )
 
                 keep(part, 24 * xh + 2 * i, 64, factor_dot(ys, jnp.concatenate(pair_of(column), axis=1)))
@@ -181,7 +195,7 @@
             def body(i):
                 def column(j):
                     at = x_rows(2 * i + j)
-                    return jnp.concatenate([lo[s, at, :], own[s, at, :], own[4 + s, at, :]], axis=0)
+                    return jnp.concatenate([near[s, at, :], own[s, at, :], own[4 + s, at, :]], axis=0)
 
                 keep(part, 8 * s + 2 * i, 96, factor_dot(xs, jnp.concatenate(pair_of(column), axis=1)))
 
@@ -211,44 +225,53 @@
             for j in range(2):
                 y = 2 * i + j
                 p = part_rows(part, 8 * s + y, 96)
-                emit(s, y, (p[:48], p[48:] + r[:, 128 * j : 128 * j + 128]))
+                p = p + r[:, 128 * j : 128 * j + 128]
+                emit(s, y, (p[:48], p[48:]))
 
         loop(4, X_UNROLL, body)
 
 
-def pick_kernel(own, y_ref, plus, minus, ym, xm, xu):
+def pick_kernel(own, y_ref, early, late_send, ym, xm, xu):
     core = core_of()
     slab = lax.div(lax.axis_index("grp"), 4)
     ny = y_ref.shape[0]
+    along_y, along_z = parities()
+    block = lambda k: lambda: own[k, pl.ds(0, ROWS), :]
+
     @pl.when(core == 0)
     def _():
-        for i, (p, m) in enumerate(((1, 0), (2, 1), (3, 2), (5, 4), (6, 5), (7, 6))):
-            plus[i] = own[p, pl.ds(0, ROWS), :]
-            minus[i] = own[m, pl.ds(0, ROWS), :]
+        put(early, late_send, along_z, [block(k) for k in (1, 2, 3, 5, 6, 7)], [block(k) for k in (0, 1, 2, 4, 5, 6)])
 
     @pl.when(core == 1)
     def _():
-        for s in range(4):
-            plus[s] = own[4 + s, pl.ds(0, ROWS), :]
-            minus[s] = own[s, pl.ds(0, ROWS), :]
-
+        put(early, late_send, along_y, [block(k) for k in (4, 5, 6, 7)], [block(k) for k in (0, 1, 2, 3)])
+
+    head = lax.broadcasted_iota(jnp.int32, (12, 256), 1) < 48
     few = lax.broadcasted_iota(jnp.int32, (12, 128), 1) < 16
     for xh in range(2):
         for s in range(4):
             p = own[4 * xh + s, pl.ds(ROWS, 12), :]
             q = jnp.where(few, own[4 * xh + s, pl.ds(ROWS + 12, 12), :], 0.0)
             w = jnp.concatenate([p, q], axis=1)
-            xm[pl.ds(48 * xh + 12 * s, 12), :] = pltpu.roll(w, 48, 1) if xh else w
+            at = pl.ds(48 * xh + 12 * s, 12)
+            here = w if xh == 0 else pltpu.roll(w, 48, 1)
+            other = jnp.zeros_like(w) if xh == 0 else pltpu.roll(w, 160, 1)
+            xm[at, :] = jnp.where(jnp.logical_and(head, along_y == 0), other, here)
+            late = (w[:, :128], jnp.zeros((12, 128), jnp.float32))
             if xh:
-                xu[pl.ds(12 * s, 12), :] = pltpu.roll(w, 160, 1)[:, :128]
+                late = (late[1], other[:, :128])
+            xu[at, :] = jnp.where(along_y == 0, late[0], late[1])
     rows = y_ref[pl.ds(pl.multiple_of(64 * slab, 64), 64), :]
-    for i, first in enumerate((-48, 64)):
-        shift = lax.rem(2 * ny - first - 64 * slab, ny)
-        ym[:, pl.ds(128 * i, 128)] = pltpu.roll(rows, shift, 1)[:, :128]
-
-
-def first_kernel(part, hi, ym, xu, out, plus, minus):
+    down, up = [pltpu.roll(rows, lax.rem(2 * ny - k - 64 * slab, ny), 1)[:, :128] for k in (-48, 64)]
+    head = lax.broadcasted_iota(jnp.int32, (64, 128), 1) < 48
+    ym[:, pl.ds(0, 128)] = jnp.where(jnp.logical_and(head, along_z == 0), up, down)
+    ym[:, pl.ds(128, 128)] = jnp.where(along_z == 0, down, up)
+
+
+def first_kernel(part, hi, ym, xu, out, early, late_send):
     core = core_of()
+    along_y, along_z = parities()
+    block = lambda k: lambda: out[k]
 
     @pl.when(core == 0)
     def _():
@@ -259,9 +282,7 @@
                     out[4 * xh + s, pl.ds(24 * h + xx, 8, stride=48), :] = w[h]
 
         y_finish(part, hi, ym, emit)
-        for s in range(4):
-            plus[s] = out[4 + s]
-            minus[s] = out[s]
+        put(early, late_send, along_y, [block(k) for k in (4, 5, 6, 7)], [block(k) for k in (0, 1, 2, 3)])
 
     @pl.when(core == 1)
     def _():
@@ -272,10 +293,7 @@
                     out[4 * xh + s, pl.ds(8 * yh + yy, 24, stride=16), :] = q[yh]
 
         x_finish(part, hi, xu, emit)
-        for xh in range(2):
-            for s in range(3):
-                plus[3 * xh + s] = out[4 * xh + s + 1]
-                minus[3 * xh + s] = out[4 * xh + s]
+        put(early, late_send, along_z, [block(k) for k in (1, 2, 3, 5, 6, 7)], [block(k) for k in (0, 1, 2, 4, 5, 6)])
 
 
 def second_kernel(part, hi, ym, xu, out):
@@ -342,13 +360,13 @@
 
     everyone = [(y, xh, z, r) for y in range(n_y) for xh in range(2) for z in range(n_z) for r in range(4)]
 
-    def hop(step, along_z):
+    def hop(turn, along_z):
         pairs = []
         for y, xh, z, r in everyone:
             if r % 2 == along_z:
-                to = place(y, xh, z + step, r)
+                to = place(y, xh, z + (1 if z % 2 == turn else -1), r)
             else:
-                to = place(y + step, xh, z, r)
+                to = place(y + (1 if y % 2 == turn else -1), xh, z, r)
             pairs.append((place(y, xh, z, r), to))
         return pairs
 
@@ -370,18 +388,18 @@
     )
     got = lax.all_to_all(sent, AXES, split_axis=0, concat_axis=0, tiled=True, axis_index_groups=eights)
 
-    plus, minus, ym, xm, xu = call(
-        pick_kernel, [(6, ROWS, 128), (6, ROWS, 128), (64, 256), (96, 256), (48, 128)], got, y_factor
+    early, late_send, ym, xm, xu = call(
+        pick_kernel, [(6, ROWS, 128), (6, ROWS, 128), (64, 256), (96, 256), (96, 128)], got, y_factor
     )
-    lo = lax.ppermute(plus, AXES, hop(1, 0))
-    hi = lax.ppermute(minus, AXES, hop(-1, 0))
-    (part,) = call(functools.partial(lower_kernel, 0), [(8 * ROWS, 128)], got, lo, ym, xm)
-    own, plus, minus = call(
+    near = lax.ppermute(early, AXES, hop(0, 0))
+    hi = lax.ppermute(late_send, AXES, hop(1, 0))
+    (part,) = call(functools.partial(lower_kernel, 0), [(8 * ROWS, 128)], got, near, ym, xm)
+    own, early, late_send = call(
         first_kernel, [(8, ROWS, 128), (6, ROWS, 128), (6, ROWS, 128)], part, hi, ym, xu
     )
-    lo = lax.ppermute(plus, AXES, hop(1, 1))
-    hi = lax.ppermute(minus, AXES, hop(-1, 1))
-    (part,) = call(functools.partial(lower_kernel, 1), [(8 * ROWS, 128)], own, lo, ym, xm)
+    near = lax.ppermute(early, AXES, hop(0, 1))
+    hi = lax.ppermute(late_send, AXES, hop(1, 1))
+    (part,) = call(functools.partial(lower_kernel, 1), [(8 * ROWS, 128)], own, near, ym, xm)
     (sent,) = call(second_kernel, [(8, ROWS, 128)], part, hi, ym, xu)
     got = lax.all_to_all(sent, AXES, split_axis=0, concat_axis=0, tiled=True, axis_index_groups=eights)
     (out,) = call(last_kernel, [(768, 512)], got, scaling.reshape(768, 512), plain=True)

time: 112 us -> 113 us (level)
  the two profiles are of different devices: /device:TPU:24 before, /device:TPU:1 now
where the time goes in v6:
time: 113 us
  blocking collectives  60.7 us (54%)
  waiting for transfers between devices  28.8 us (25%)
  starting transfers between devices  14.4 us (13%)
  Pallas kernels  8.48 us (8%)
    all_to_all x2, blocking collectives, on_device(): lax.all_to_all(sent, AXES, split_axis=0, concat_axis=0, tiled=True, axis_...  60.7 us
    ppermute x1, waiting for transfers between devices, on_device(): near = lax.ppermute(early, AXES, hop(0, 0))  13.4 us
    ppermute x1, starting transfers between devices, on_device(): hi = lax.ppermute(late_send, AXES, hop(1, 1))  8.59 us
    pallas_call x7, Pallas kernels, call(): pl.pallas_call(kernel, out_shape=outs, in_specs=[pl.BlockSpec(memory_spac...  8.48 us
    ppermute x1, waiting for transfers between devices, on_device(): near = lax.ppermute(early, AXES, hop(0, 1))  6.71 us
    ppermute x1, waiting for transfers between devices, on_device(): hi = lax.ppermute(late_send, AXES, hop(1, 1))  6.38 us
    ppermute x1, waiting for transfers between devices, on_device(): hi = lax.ppermute(late_send, AXES, hop(1, 0))  2.37 us
  transfers between devices with their start and end apart: 4, of which 4 were waited for; matrix products, arithmetic and copies ran while one was open for 0% of the time, Pallas kernels for 1%

profile of v6, /device:TPU:1, one launch (start us, length us, event | category | flops | bytes accessed | tf_op | source)
XLA Modules:
  0.0 112.5 jit_solution(8575820721946912034)
XLA Ops:
  0.0 3.2 %shard_map.55 = f32[8,408,128]{2,1,0:T(8,128)S(1)} custom-call(f32[768,512]{1,0:T(8,128)} %bitcast.4, f32[512,512]{1,0:T(8,128)} %z_hbm.1, f32[48,144]{1,0:T(8,128)} %panel_hbm.1), custom_call_target="tpu_custom_call" | custom-call | tf_op jit(solution)/shard_map/pallas_call | solution.py:343
  3.2 0.0 copy-start
  3.2 34.8 %all_to_all.10.own = f32[8,408,128]{2,1,0:T(8,128)S(1)} all-to-all(f32[8,408,128]{2,1,0:T(8,128)S(1)} %shard_map.55), channel_id=1, replica_groups={{0,1,2,3,48,49,50,51},{4,5,6,7,52,53,54,55},{8,9,10,11,56,57,58,59},{12..., dimensions={0} | all-to-all | bytes 3342336 | tf_op jit(solution)/shard_map/all_to_all | solution.py:389
  38.1 0.0 copy-done
  38.1 0.3 shard_map.56
  38.4 1.9 %collective-permute-start = (f32[6,384,128]{2,1,0:T(8,128)S(1)}, f32[6,384,128]{2,1,0:T(8,128)S(1)}, u32[]{:S(2)}, u32[]{:S(2)}) collective-permute-start(f32[6,384,128]{2,1,0:T(8,128)S(1)} %get-tuple-element.13), channel_id=1, source_target_pairs={{0,4},{1,97},{2,6},{3,99},{4,0},{5,101},{6,2},{7,103},{8,12},{9,10... | collective-permute-start | bytes 3538952 | tf_op jit(solution)/shard_map/ppermute | solution.py:394
  40.3 1.9 %collective-permute-start.1 = (f32[6,384,128]{2,1,0:T(8,128)S(1)}, f32[6,384,128]{2,1,0:T(8,128)S(1)}, u32[]{:S(2)}, u32[]{:S(2)}) collective-permute-start(f32[6,384,128]{2,1,0:T(8,128)S(1)} %get-tuple-element.16), channel_id=1, source_target_pairs={{0,44},{1,673},{2,46},{3,675},{4,8},{5,677},{6,10},{7,679},{8,4},{... | collective-permute-start | bytes 3538952 | tf_op jit(solution)/shard_map/ppermute | solution.py:395
  42.2 13.4 %collective-permute-done.near = f32[6,384,128]{2,1,0:T(8,128)S(1)} collective-permute-done((f32[6,384,128]{2,1,0:T(8,128)S(1)}, f32[6,384,128]{2,1,0:T(8,128)S(1)}, u32[]{:S(2)}, u32[]{:S(2)}) %collective-permute-start) | collective-permute-done | bytes 1179680 | tf_op jit(solution)/shard_map/ppermute | solution.py:394
  55.6 0.8 shard_map.57.part
  56.4 2.4 %collective-permute-done.1.hi = f32[6,384,128]{2,1,0:T(8,128)S(1)} collective-permute-done((f32[6,384,128]{2,1,0:T(8,128)S(1)}, f32[6,384,128]{2,1,0:T(8,128)S(1)}, u32[]{:S(2)}, u32[]{:S(2)}) %collective-permute-start.1) | collective-permute-done | bytes 1179680 | tf_op jit(solution)/shard_map/ppermute | solution.py:395
  58.8 1.1 shard_map.58
  59.8 1.9 %collective-permute-start.2 = (f32[6,384,128]{2,1,0:T(8,128)S(1)}, f32[6,384,128]{2,1,0:T(8,128)S(1)}, u32[]{:S(2)}, u32[]{:S(2)}) collective-permute-start(f32[6,384,128]{2,1,0:T(8,128)S(1)} %get-tuple-element.19), channel_id=1, source_target_pairs={{0,96},{1,5},{2,98},{3,7},{4,100},{5,1},{6,102},{7,3},{8,104},{9,1... | collective-permute-start | bytes 3538952 | tf_op jit(solution)/shard_map/ppermute | solution.py:400
  61.8 8.6 %collective-permute-start.3 = (f32[6,384,128]{2,1,0:T(8,128)S(1)}, f32[6,384,128]{2,1,0:T(8,128)S(1)}, u32[]{:S(2)}, u32[]{:S(2)}) collective-permute-start(f32[6,384,128]{2,1,0:T(8,128)S(1)} %get-tuple-element.20), channel_id=1, source_target_pairs={{0,672},{1,45},{2,674},{3,47},{4,676},{5,9},{6,678},{7,11},{8,680}... | collective-permute-start | bytes 3538952 | tf_op jit(solution)/shard_map/ppermute | solution.py:401
  70.4 6.7 %collective-permute-done.2.near = f32[6,384,128]{2,1,0:T(8,128)S(1)} collective-permute-done((f32[6,384,128]{2,1,0:T(8,128)S(1)}, f32[6,384,128]{2,1,0:T(8,128)S(1)}, u32[]{:S(2)}, u32[]{:S(2)}) %collective-permute-start.2) | collective-permute-done | bytes 1179680 | tf_op jit(solution)/shard_map/ppermute | solution.py:400
  77.1 0.8 shard_map.59.part
  77.9 6.4 %collective-permute-done.3.hi = f32[6,384,128]{2,1,0:T(8,128)S(1)} collective-permute-done((f32[6,384,128]{2,1,0:T(8,128)S(1)}, f32[6,384,128]{2,1,0:T(8,128)S(1)}, u32[]{:S(2)}, u32[]{:S(2)}) %collective-permute-start.3) | collective-permute-done | bytes 1179680 | tf_op jit(solution)/shard_map/ppermute | solution.py:401
  84.2 0.8 shard_map.60
  85.0 0.0 copy-start.1
  85.0 25.9 %all_to_all.11.got = f32[8,384,128]{2,1,0:T(8,128)S(1)} all-to-all(f32[8,384,128]{2,1,0:T(8,128)S(1)} %shard_map.60), channel_id=1, replica_groups={{0,1,2,3,48,49,50,51},{4,5,6,7,52,53,54,55},{8,9,10,11,56,57,58,59},{12..., dimensions={0} | all-to-all | bytes 3145728 | tf_op jit(solution)/shard_map/all_to_all | solution.py:404
  110.9 0.0 copy-done.1
  110.9 1.6 %shard_map.61 = f32[768,512]{1,0:T(8,128)} custom-call(f32[8,384,128]{2,1,0:T(8,128)S(1)} %all_to_all.11.got, f32[768,512]{1,0:T(8,128)S(1)} %bitcast.3), custom_call_target="tpu_custom_call" | custom-call | tf_op jit(solution)/shard_map/pallas_call | solution.py:343
Async XLA Ops:
  3.2 34.9 %copy-start = (f32[768,768]{1,0:T(8,128)S(1)}, f32[768,768]{1,0:T(8,128)}, u32[]{:S(2)}) copy-start(f32[768,768]{1,0:T(8,128)} %y_ref.1) | copy-start | bytes 7077892
  38.4 17.2 %collective-permute-start = (f32[6,384,128]{2,1,0:T(8,128)S(1)}, f32[6,384,128]{2,1,0:T(8,128)S(1)}, u32[]{:S(2)}, u32[]{:S(2)}) collective-permute-start(f32[6,384,128]{2,1,0:T(8,128)S(1)} %get-tuple-element.13), channel_id=1, source_target_pairs={{0,4},{1,97},{2,6},{3,99},{4,0},{5,101},{6,2},{7,103},{8,12},{9,10... | collective-permute-start | bytes 3538952 | tf_op jit(solution)/shard_map/ppermute | solution.py:394
  40.3 18.5 %collective-permute-start.1 = (f32[6,384,128]{2,1,0:T(8,128)S(1)}, f32[6,384,128]{2,1,0:T(8,128)S(1)}, u32[]{:S(2)}, u32[]{:S(2)}) collective-permute-start(f32[6,384,128]{2,1,0:T(8,128)S(1)} %get-tuple-element.16), channel_id=1, source_target_pairs={{0,44},{1,673},{2,46},{3,675},{4,8},{5,677},{6,10},{7,679},{8,4},{... | collective-permute-start | bytes 3538952 | tf_op jit(solution)/shard_map/ppermute | solution.py:395
  59.8 17.2 %collective-permute-start.2 = (f32[6,384,128]{2,1,0:T(8,128)S(1)}, f32[6,384,128]{2,1,0:T(8,128)S(1)}, u32[]{:S(2)}, u32[]{:S(2)}) collective-permute-start(f32[6,384,128]{2,1,0:T(8,128)S(1)} %get-tuple-element.19), channel_id=1, source_target_pairs={{0,96},{1,5},{2,98},{3,7},{4,100},{5,1},{6,102},{7,3},{8,104},{9,1... | collective-permute-start | bytes 3538952 | tf_op jit(solution)/shard_map/ppermute | solution.py:400
  61.8 22.5 %collective-permute-start.3 = (f32[6,384,128]{2,1,0:T(8,128)S(1)}, f32[6,384,128]{2,1,0:T(8,128)S(1)}, u32[]{:S(2)}, u32[]{:S(2)}) collective-permute-start(f32[6,384,128]{2,1,0:T(8,128)S(1)} %get-tuple-element.20), channel_id=1, source_target_pairs={{0,672},{1,45},{2,674},{3,47},{4,676},{5,9},{6,678},{7,11},{8,680}... | collective-permute-start | bytes 3538952 | tf_op jit(solution)/shard_map/ppermute | solution.py:401
  85.0 25.9 %copy-start.1 = (f32[16,48,512]{2,1,0:T(8,128)S(1)}, f32[16,48,512]{2,1,0:T(8,128)}, u32[]{:S(2)}) copy-start(f32[16,48,512]{2,1,0:T(8,128)} %param.9) | copy-start | bytes 4718596
